TPU v7x, 128 devices: a whole 4x4x4 slice. The times are simulated.
128 devices in a mesh: slab: 8 (over y, core), ray: 16 (over z, x).
Axes of the slice: x: 4, y: 4, z: 4, core: 2. Of those that a mesh axis runs over, the one named last changes fastest.
Arguments:
- intensity: float32 [8, 16, 256, 2048], P('slab', 'ray'), may hold values from 0.2 to 1
- angles: float32 [8, 16], replicated, may hold values from 0 to 3.14159
- volume: float32 [256, 64, 256], P('slab', 'ray'), may hold values from -3 to 3
- vol_list: int32 [64], replicated, may hold values from 0 to 63, as said below
Outputs:
- reconstruction: float32 [256, 64, 256], P('slab', 'ray')
- residual: float32 [8, 16, 256, 2048], P(None, 'ray', 'slab')
Inputs may be any that keep to these rules, and one draw needn't show every extreme that they name: vol_list is a permutation of the patch ids that follows a Hilbert curve over the 8 x 8 grid of patches.
All inputs are finite; a program needn't handle non-finite values.
Results may differ from a plain program's by a relative error of at most 0.0003.
Values sent between devices are 32-bit elements; how exact they have to be, the bound alone decides.
A program may use at most 192 MiB of HBM per device.

v0:
```python
import math

import jax
import jax.numpy as jnp
from jax import lax
from jax.sharding import PartitionSpec as P

BAND = 2048
TR = 32
PGRID = 8
ROI = 128


paganin_strength = 10.0
relax = 1.8
row_floor = 0.25
highest = lax.Precision.HIGHEST


def split_length(length):
    return max((divisor for divisor in range(1, math.isqrt(length) + 1) if length % divisor == 0))


def phase_table(count_a, count_b, total):
    index_a = jnp.arange(count_a, dtype=jnp.int32)[:, None]
    index_b = jnp.arange(count_b, dtype=jnp.int32)[None, :]
    phases = (index_a * index_b % total).astype(jnp.float32) * (2.0 * jnp.pi / total)
    return (jnp.cos(phases), jnp.sin(phases))


def permuted_freq(length, outer):
    inner = length // outer
    position = jnp.arange(length, dtype=jnp.int32)
    return position // inner + outer * (position % inner)


def gain_values(row_freq, col_freq, height, width_px):
    row_part = 2.0 - 2.0 * jnp.cos(2.0 * jnp.pi * row_freq.astype(jnp.float32) / height)
    col_part = 2.0 - 2.0 * jnp.cos(2.0 * jnp.pi * col_freq.astype(jnp.float32) / width_px)
    return 1.0 / (1.0 + paganin_strength * (row_part[:, None] + col_part[None, :]))


def cols_outer(table, values):
    return jnp.einsum("kn,asnm->askm", table, values, precision=highest)


def cols_inner(values, table):
    return jnp.einsum("askm,ml->askl", values, table, precision=highest)


def rows_outer(table, values):
    return jnp.einsum("kn,anmc->akmc", table, values, precision=highest)


def rows_inner(table, values):
    return jnp.einsum("lm,akmc->aklc", table, values, precision=highest)


def paganin(images):
    num_images, height, width_px = images.shape
    inner_cols = min(width_px, 128)
    outer_cols = width_px // inner_cols
    outer_rows = split_length(height)
    inner_rows = height // outer_rows
    col_outer_cos, col_outer_sin = phase_table(outer_cols, outer_cols, outer_cols)
    col_turn_cos, col_turn_sin = phase_table(outer_cols, inner_cols, width_px)
    col_inner_cos, col_inner_sin = phase_table(inner_cols, inner_cols, inner_cols)
    row_outer_cos, row_outer_sin = phase_table(outer_rows, outer_rows, outer_rows)
    row_turn_cos, row_turn_sin = phase_table(outer_rows, inner_rows, height)
    row_turn_cos = row_turn_cos[None, :, :, None]
    row_turn_sin = row_turn_sin[None, :, :, None]
    row_inner_cos, row_inner_sin = phase_table(inner_rows, inner_rows, inner_rows)
    col_shape = (num_images, height, outer_cols, inner_cols)
    row_shape = (num_images, outer_rows, inner_rows, width_px)
    pieces = images.reshape(col_shape)
    first_real = cols_outer(col_outer_cos, pieces)
    first_imag = -cols_outer(col_outer_sin, pieces)
    turned_real = first_real * col_turn_cos + first_imag * col_turn_sin
    turned_imag = first_imag * col_turn_cos - first_real * col_turn_sin
    col_real = (
        cols_inner(turned_real, col_inner_cos) + cols_inner(turned_imag, col_inner_sin)
    ).reshape(row_shape)
    col_imag = (
        cols_inner(turned_imag, col_inner_cos) - cols_inner(turned_real, col_inner_sin)
    ).reshape(row_shape)
    row_real = rows_outer(row_outer_cos, col_real) + rows_outer(row_outer_sin, col_imag)
    row_imag = rows_outer(row_outer_cos, col_imag) - rows_outer(row_outer_sin, col_real)
    mixed_real = row_real * row_turn_cos + row_imag * row_turn_sin
    mixed_imag = row_imag * row_turn_cos - row_real * row_turn_sin
    gain_table = gain_values(
        permuted_freq(height, outer_rows), permuted_freq(width_px, outer_cols), height, width_px
    ).reshape(1, outer_rows, inner_rows, width_px)
    spec_real = (
        rows_inner(row_inner_cos, mixed_real) + rows_inner(row_inner_sin, mixed_imag)
    ) * gain_table
    spec_imag = (
        rows_inner(row_inner_cos, mixed_imag) - rows_inner(row_inner_sin, mixed_real)
    ) * gain_table
    back_real = rows_inner(row_inner_cos, spec_real) - rows_inner(row_inner_sin, spec_imag)
    back_imag = rows_inner(row_inner_cos, spec_imag) + rows_inner(row_inner_sin, spec_real)
    reverted_real = back_real * row_turn_cos - back_imag * row_turn_sin
    reverted_imag = back_imag * row_turn_cos + back_real * row_turn_sin
    rows_real = (
        rows_outer(row_outer_cos, reverted_real) - rows_outer(row_outer_sin, reverted_imag)
    ).reshape(col_shape)
    rows_imag = (
        rows_outer(row_outer_cos, reverted_imag) + rows_outer(row_outer_sin, reverted_real)
    ).reshape(col_shape)
    last_real = cols_inner(rows_real, col_inner_cos) - cols_inner(rows_imag, col_inner_sin)
    last_imag = cols_inner(rows_imag, col_inner_cos) + cols_inner(rows_real, col_inner_sin)
    final_real = last_real * col_turn_cos - last_imag * col_turn_sin
    final_imag = last_imag * col_turn_cos + last_real * col_turn_sin
    result = (
        cols_outer(col_outer_cos, final_real) - cols_outer(col_outer_sin, final_imag)
    ).reshape(num_images, height, width_px)
    offset = (width_px - BAND) // 2
    return result / (height * width_px)


def mat_dot(left_op, right_op):
    return jnp.dot(left_op, right_op, precision=highest, preferred_element_type=jnp.float32)


def ray_windows(patch_ids, theta):
    half_roi = (ROI - 1) / 2.0
    half_band = (BAND - 1) / 2.0
    centre_x = (patch_ids // PGRID).astype(jnp.float32) * 16.0 + 7.5 - half_roi
    centre_y = (patch_ids % PGRID).astype(jnp.float32) * 16.0 + 7.5 - half_roi
    centre = (
        half_band
        + centre_x[:, None] * jnp.cos(theta)[None, :]
        + centre_y[:, None] * jnp.sin(theta)[None, :]
    )
    starts = jnp.floor(centre).astype(jnp.int32) - 15
    return starts[:, :, None] + jnp.arange(TR, dtype=jnp.int32)[None, None, :]


def tile_weights(patch_id, theta):
    half_roi = (ROI - 1) / 2.0
    half_band = (BAND - 1) / 2.0
    ray_index = ray_windows(jnp.reshape(patch_id, (1,)), theta)[0]
    voxels = jnp.arange(256, dtype=jnp.int32)
    voxel_x = (
        (patch_id // PGRID).astype(jnp.float32) * 16.0
        + (voxels // 16).astype(jnp.float32)
        - half_roi
    )
    voxel_y = (
        (patch_id % PGRID).astype(jnp.float32) * 16.0 + (voxels % 16).astype(jnp.float32) - half_roi
    )
    cosine = jnp.cos(theta)
    sine = jnp.sin(theta)
    along = (
        voxel_x[:, None, None] * cosine[None, :, None]
        + voxel_y[:, None, None] * sine[None, :, None]
    )
    distance = (ray_index.astype(jnp.float32) - half_band)[None, :, :] - along
    weights = jnp.maximum(0.0, 1.0 - jnp.abs(distance)) / ROI
    return (weights.reshape(256, -1), ray_index)


def window_index(starts):
    num_angles = starts.shape[1]
    window_lane = jnp.arange(TR, dtype=jnp.int32)
    angle_base = jnp.arange(num_angles, dtype=jnp.int32) * BAND
    return (angle_base[None, :, None] + starts[:, :, None] + window_lane[None, None, :]).reshape(-1)


def place_windows(tiles, starts):
    num_rows = tiles.shape[0]
    num_angles = starts.shape[1]
    flat_index = window_index(starts)
    empty = jnp.zeros((num_rows, num_angles * BAND), jnp.float32)
    return empty.at[:, flat_index].add(tiles.reshape(num_rows, -1))


def take_windows(values, starts):
    flat_index = window_index(starts)
    return values[:, flat_index].reshape(values.shape[0], starts.shape[0], starts.shape[1], TR)


def local(intensity, angles, volume, vol_list):
    per_device = intensity.shape[0]
    n_slab = lax.axis_size("slab")
    n_ray = lax.axis_size("ray")
    slab_rows = intensity.shape[2] // n_slab
    images = intensity.reshape(per_device, intensity.shape[2], intensity.shape[3])
    projected = -jnp.log(paganin(images))
    pieces = projected.reshape(per_device, n_slab, slab_rows, BAND)
    moved = lax.all_to_all(pieces, "slab", split_axis=1, concat_axis=0, tiled=True)
    own_count = moved.shape[0]
    sinogram = jnp.transpose(moved[:, 0], (1, 0, 2)).reshape(slab_rows, own_count * BAND)
    rank = lax.axis_index("ray")
    theta_own = lax.dynamic_index_in_dim(angles, rank, 1, keepdims=False)
    slots = volume.shape[1]
    num_patches = vol_list.shape[0]
    step_size = relax * ROI / (angles.shape[0] * angles.shape[1])
    starts = ray_windows(vol_list, theta_own)[:, :, 0]
    my_ids = lax.dynamic_slice_in_dim(vol_list, rank * slots, slots)
    theta_all = jnp.transpose(angles).reshape(-1)

    def forward(current, with_sums):
        values = []
        sums = []
        for slot_idx in range(slots):
            weights, _ = tile_weights(my_ids[slot_idx], theta_all)
            values.append(mat_dot(current[:, slot_idx, :], weights))
            if with_sums:
                sums.append(jnp.sum(weights, axis=0))
        stacked = jnp.stack(values, axis=1).reshape(slab_rows, slots, n_ray, own_count * TR)
        if with_sums:
            sum_rows = jnp.stack(sums, axis=0).reshape(1, slots, n_ray, own_count * TR)
            got_vals, got_sums = (
                lax.all_to_all(stacked, "ray", split_axis=2, concat_axis=1, tiled=True),
                lax.all_to_all(sum_rows, "ray", split_axis=2, concat_axis=1, tiled=True),
            )
            tiles = jnp.concatenate(
                [
                    got_vals.reshape(slab_rows, num_patches, own_count, TR),
                    got_sums.reshape(1, num_patches, own_count, TR),
                ],
                axis=0,
            )
            placed = place_windows(tiles, starts)
            return (placed[:slab_rows], placed[slab_rows])
        got_vals = lax.all_to_all(stacked, "ray", split_axis=2, concat_axis=1, tiled=True)
        return (
            place_windows(got_vals.reshape(slab_rows, num_patches, own_count, TR), starts),
            None,
        )

    def backward(scaled):
        windows = take_windows(scaled, starts).reshape(slab_rows, num_patches, 1, own_count * TR)
        got_back = lax.all_to_all(windows, "ray", split_axis=1, concat_axis=2, tiled=True).reshape(
            slab_rows, slots, -1
        )
        updates = []
        for slot_idx in range(slots):
            weights, _ = tile_weights(my_ids[slot_idx], theta_all)
            updates.append(
                lax.dot_general(
                    got_back[:, slot_idx, :],
                    weights,
                    (((1,), (1,)), ((), ())),
                    precision=highest,
                    preferred_element_type=jnp.float32,
                )
            )
        return jnp.stack(updates, axis=1)

    predicted, row_sums = forward(volume, True)
    row_weight = 1.0 / jnp.maximum(row_sums, row_floor)
    difference = sinogram - predicted
    first_iterate = volume + step_size * backward(difference * row_weight[None, :])
    predicted_next, _ = forward(first_iterate, False)
    residual = sinogram - predicted_next
    reconstruction = first_iterate + step_size * backward(residual * row_weight[None, :])
    residual_out = jnp.transpose(residual.reshape(slab_rows, own_count, BAND), (1, 0, 2))[:, None]
    return (reconstruction, residual_out)


def solution(mesh):
    placed = (P("slab", "ray", None, None), P(), P("slab", "ray", None), P())
    return jax.shard_map(
        local,
        mesh=mesh,
        in_specs=placed,
        out_specs=(P("slab", "ray", None), P(None, "ray", "slab", None)),
        check_vma=False,
    )
```

profile of v0, /device:TPU:0, one launch (start us, length us, event | category | flops | bytes accessed | tf_op | source)
XLA Modules:
  0.0 745.5 jit_solution(8702745690804195368)
XLA Ops:
  24.2 5.6 maximum_multiply_fusion.1
  30.1 5.6 maximum_multiply_fusion.3
  36.5 8.2 %all-to-all-start.2 = ((f32[1,4,16,256]{3,1,0,2:T(4,128)}), f32[1,4,16,256]{3,1,0,2:T(4,128)}, u32[]{:S(2)}, u32[]{:S(2)}) async-start(f32[1,4,16,256]{3,1,0,2:T(4,128)} %copy.216), calls=%async_computation.2 | async-start | bytes 131072 | tf_op jit(solution)/shard_map/all_to_all | solution.py:215
  64.2 6.1 fusion.63
  78.9 4.5 fusion.67
  83.4 6.3 fusion.29
  89.8 6.1 subtract_bitcast_fusion.1
  163.9 4.5 all-to-all-start
  168.4 6.2 fusion.114
  175.9 4.7 fusion.111
  189.1 6.5 all-to-all-done
  195.6 7.4 all-to-all-start.1
  204.0 4.7 copy.203
  208.7 25.3 %all-to-all-done.1 = f32[32,4,16,256]{3,0,1,2:T(8,128)} async-done(((f32[32,4,16,256]{3,0,1,2:T(8,128)}), f32[32,4,16,256]{3,0,1,2:T(8,128)}, u32[]{:S(2)}, u32[]{:S(2)}) %all-to-all-start.1) | async-done | bytes 2097184 | tf_op jit(solution)/shard_map/all_to_all | solution.py:214
  240.9 4.8 copy.217
  245.6 91.4 %scatter_custom_fusion = f32[33,16384]{0,1:T(8,128)} fusion(s32[16384]{0:T(1024)S(1)} %bitcast.459, f32[16384,33]{1,0:T(8,128)} %copy.217, f32[]{:T(128)} %constant.548.clone.1), kind=kCustom, calls=%fused_computation.37 | custom fusion | flops 540672 | bytes 2163200 | tf_op jit(solution)/shard_map/scatter-add | solution.py:174
  337.0 7.6 %fusion.2 = f32[16384]{0:T(1024)S(1)} fusion(f32[33,16384]{0,1:T(8,128)} %scatter_custom_fusion), kind=kLoop, calls=%fused_computation.9 | loop fusion | flops 32768 | bytes 131072 | tf_op jit(solution)/shard_map/div | solution.py:252
  344.6 7.9 %fusion.1 = f32[32,16384]{0,1:T(8,128)} fusion(f32[33,16384]{0,1:T(8,128)S(1)} %copy-done, f32[32,8,2048]{0,2,1:T(8,128)} %copy.203, f32[16384]{0:T(1024)S(1)} %fusion.2), kind=kLoop, calls=%fused_computation.7 | loop fusion | flops 1048576 | bytes 6356992 | tf_op jit(solution)/shard_map/mul | solution.py:254
  352.5 57.8 %gather_fusion = f32[16384,32]{1,0:T(8,128)} fusion(f32[32,16384]{0,1:T(8,128)} %fusion.1, s32[16384]{0:T(1024)S(1)} %broadcast_clamp_fusion), kind=kCustom, calls=%fused_computation | custom fusion | bytes 4259840 | tf_op jit(solution)/shard_map/gather | solution.py:179
  410.3 6.2 copy.218
  420.8 4.1 fusion.14
  428.9 21.8 %all-to-all-done.3 = f32[32,64,1,256]{3,0,2,1:T(8,128)S(1)} async-done(((f32[32,64,1,256]{3,0,2,1:T(8,128)}), f32[32,64,1,256]{3,0,2,1:T(8,128)S(1)}, u32[]{:S(2)}, u32[]{:S(2)}) %all-to-all-start.3) | async-done | bytes 2097184 | tf_op jit(solution)/shard_map/all_to_all | solution.py:234
  455.5 4.4 convolution_bitcast_fusion.11
  482.8 31.6 %all_to_all.84 = f32[32,4,16,256]{3,0,1,2:T(8,128)S(1)} all-to-all(f32[32,4,16,256]{3,0,1,2:T(8,128)S(1)} %copy.221), channel_id=1, replica_groups=mesh['slab'=8,'ray'=16] {'ray'}, dimensions={2} | all-to-all | bytes 4194304 | tf_op jit(solution)/shard_map/all_to_all | solution.py:226
  519.4 4.6 copy.223
  524.1 91.4 %scatter_custom_fusion.1 = f32[32,16384]{0,1:T(8,128)} fusion(s32[16384]{0:T(1024)S(1)} %bitcast.460, f32[16384,32]{1,0:T(8,128)} %copy.223, f32[]{:T(128)} %constant.548.clone.1), kind=kCustom, calls=%fused_computation.30 | custom fusion | flops 524288 | bytes 2097664 | tf_op jit(solution)/shard_map/scatter-add | solution.py:174
  615.4 16.0 %broadcast_multiply_fusion = (f32[32,16384]{0,1:T(8,128)}, f32[32,16384]{0,1:T(8,128)}) fusion(f32[16384]{0:T(1024)S(1)} %fusion.2, f32[32,16384]{0,1:T(8,128)} %scatter_custom_fusion.1, f32[32,8,2048]{0,2,1:T(8,128)} %copy.203), kind=kLoop, calls=%fused_computation.32 | loop fusion | flops 1048576 | bytes 8454144 | tf_op jit(solution)/shard_map/mul | solution.py:257
  631.4 57.8 %gather_fusion.1 = f32[16384,32]{1,0:T(8,128)} fusion(f32[32,16384]{0,1:T(8,128)} %get-tuple-element.14, s32[16384]{0:T(1024)S(1)} %broadcast_clamp_fusion), kind=kCustom, calls=%fused_computation.1 | custom fusion | bytes 4259840 | tf_op jit(solution)/shard_map/gather | solution.py:179
  689.2 6.2 copy.224
  699.4 6.2 copy.226
  705.7 23.6 %all-to-all-done.5 = f32[32,64,1,256]{3,0,2,1:T(8,128)S(1)} async-done(((f32[32,64,1,256]{3,0,2,1:T(8,128)}), f32[32,64,1,256]{3,0,2,1:T(8,128)S(1)}, u32[]{:S(2)}, u32[]{:S(2)}) %all-to-all-start.5) | async-done | bytes 2097184 | tf_op jit(solution)/shard_map/all_to_all | solution.py:234
  733.6 4.4 convolution_bitcast_fusion.7
  (192 shorter events, 173.6 us)
Async XLA Ops:
  23.5 6.3 copy-start.23
  23.6 6.2 copy-start.25
  24.0 6.1 copy-start.27
  24.1 6.0 copy-start.29
  24.2 5.7 copy-start.19
  30.1 14.7 %copy-start.18 = (f32[1,1,256,2048]{3,2,1,0:T(8,128)S(1)}, f32[1,1,256,2048]{3,2,1,0:T(8,128)}, u32[]{:S(2)}) copy-start(f32[1,1,256,2048]{3,2,1,0:T(8,128)} %param.4) | copy-start | bytes 6291460
  36.5 127.4 %all-to-all-start.2 = ((f32[1,4,16,256]{3,1,0,2:T(4,128)}), f32[1,4,16,256]{3,1,0,2:T(4,128)}, u32[]{:S(2)}, u32[]{:S(2)}) async-start(f32[1,4,16,256]{3,1,0,2:T(4,128)} %copy.216), calls=%async_computation.2 | async-start | bytes 131072 | tf_op jit(solution)/shard_map/all_to_all | solution.py:215
  64.2 6.1 copy-start.16
  78.9 4.5 copy-start.17
  83.4 6.4 copy-start.10
  143.4 6.3 copy-start.21
  146.4 3.4 copy-start.4
  149.7 4.0 copy-start.31
  149.8 4.0 copy-start.1
  163.9 31.7 %all-to-all-start = ((f32[1,8,32,2048]{3,2,0,1:T(8,128)}), f32[1,8,32,2048]{3,2,0,1:T(8,128)S(1)}, u32[]{:S(2)}, u32[]{:S(2)}) async-start(f32[1,8,32,2048]{3,2,0,1:T(8,128)} %bitcast.442), calls=%async_computation | async-start | bytes 4194304 | tf_op jit(solution)/shard_map/all_to_all | solution.py:190
  168.4 7.5 %copy-start.7 = (f32[256,128,32]{0,2,1:T(8,128)S(1)}, f32[256,128,32]{0,2,1:T(8,128)}, u32[]{:S(2)}) copy-start(f32[256,128,32]{0,2,1:T(8,128)} %get-tuple-element.54) | copy-start | bytes 12582916
  189.1 13.9 %copy-start.32 = (s32[16384,1]{0,1:T(1,128)S(1)}, s32[16384,1]{0,1:T(1,128)}, u32[]{:S(2)}) copy-start(s32[16384,1]{0,1:T(1,128)} %add.1196) | copy-start | bytes 196612
  195.6 38.5 %all-to-all-start.1 = ((f32[32,4,16,256]{3,0,1,2:T(8,128)}), f32[32,4,16,256]{3,0,1,2:T(8,128)}, u32[]{:S(2)}, u32[]{:S(2)}) async-start(f32[32,4,16,256]{3,0,1,2:T(8,128)} %pad_maximum_fusion), calls=%async_computation.1 | async-start | bytes 4194304 | tf_op jit(solution)/shard_map/all_to_all | solution.py:214
  337.0 7.6 %copy-start = (f32[33,16384]{0,1:T(8,128)S(1)}, f32[33,16384]{0,1:T(8,128)}, u32[]{:S(2)}) copy-start(f32[33,16384]{0,1:T(8,128)} %scatter_custom_fusion) | copy-start | bytes 6488068
  416.5 3.9 copy-start.30
  416.5 4.0 copy-start.26
  416.5 4.1 copy-start.24
  416.5 4.1 copy-start.28
  416.5 4.2 copy-start.20
  416.5 34.2 %all-to-all-start.3 = ((f32[32,64,1,256]{3,0,2,1:T(8,128)}), f32[32,64,1,256]{3,0,2,1:T(8,128)S(1)}, u32[]{:S(2)}, u32[]{:S(2)}) async-start(f32[32,64,1,256]{3,0,2,1:T(8,128)} %copy.218), calls=%async_computation.3 | async-start | bytes 4194304 | tf_op jit(solution)/shard_map/all_to_all | solution.py:234
  455.4 4.5 copy-start.5
  464.3 2.3 copy-start.13
  466.6 3.9 copy-start.12
  470.5 4.1 copy-start.15
  474.5 3.9 copy-start.14
  695.5 33.7 %all-to-all-start.5 = ((f32[32,64,1,256]{3,0,2,1:T(8,128)}), f32[32,64,1,256]{3,0,2,1:T(8,128)S(1)}, u32[]{:S(2)}, u32[]{:S(2)}) async-start(f32[32,64,1,256]{3,0,2,1:T(8,128)} %copy.224), calls=%async_computation.5 | async-start | bytes 4194304 | tf_op jit(solution)/shard_map/all_to_all | solution.py:234
  733.5 4.5 copy-start.6
  (8 other events, 15.1 us)
where the time goes:
time: 751 us; the launch traced here: 746 us
  other arithmetic  241 us (32%)
  local copies, waits for them, and re-layouts  197 us (26%)
  matrix products  149 us (20%)
  waiting for transfers between devices  77.2 us (10%)
  blocking collectives  31.6 us (4%)
  starting transfers between devices  27.9 us (4%)
  between operations  22.4 us (3%)
    scatter-add x2, other arithmetic, place_windows(): return empty.at[:, flat_index].add(tiles.reshape(num_rows, -1))  183 us
    gather x2, local copies, waits for them, and re-layouts, take_windows(): values[:, flat_index]  116 us
    all_to_all x2, waiting for transfers between devices, backward(): lax.all_to_all(windows, 'ray', split_axis=1, concat_axis=2, tiled=True)  45.4 us
    dot_general x8, matrix products, rows_outer(): return jnp.einsum('kn,anmc->akmc', table, values, precision=highest)  36.1 us
    dot_general x8, matrix products, mat_dot(): jnp.dot(left_op, right_op, precision=highest, preferred_element_type=jnp....  34.5 us
    all_to_all x1, blocking collectives, forward(): lax.all_to_all(stacked, 'ray', split_axis=2, concat_axis=1, tiled=True)  31.6 us
    all_to_all x1, waiting for transfers between devices, forward(): lax.all_to_all(stacked, 'ray', split_axis=2, concat_axis=1, tiled=True)  25.3 us
    dot_general x8, matrix products, rows_inner(): return jnp.einsum('lm,akmc->aklc', table, values, precision=highest)  23.1 us
  transfers between devices with their start and end apart: 5, of which 4 were waited for; matrix products, arithmetic and copies ran while one was open for 21% of the time, Pallas kernels for 0%

commit v1 on v0

v1 whole, which is shorter than its diff:
```python
import functools

import jax
import jax.numpy as jnp
import numpy as np
from jax import lax
from jax.experimental import pallas as pl
from jax.experimental.pallas import tpu as pltpu
from jax.sharding import PartitionSpec as P

BAND = 2048
PGRID = 8
ROI = 128
HALF_ROI = (ROI - 1) / 2.0
HALF_BAND = (BAND - 1) / 2.0
STRENGTH = 10.0
RELAX = 1.8
ROW_FLOOR = 0.25
MESH = pl.DeviceIdType.MESH

TR = 32
MID0 = 896
MID = 256
RAY0 = 928
RAYS = 192
SKIP = RAY0 - MID0
STRIDE = RAYS
LEAD = RAYS - TR
F32 = jnp.float32
BF16 = jnp.bfloat16


def dot(a, b):
    return lax.dot_general(a, b, (((1,), (0,)), ((), ())), preferred_element_type=F32)


def dot_nt(a, b):
    return lax.dot_general(a, b, (((1,), (1,)), ((), ())), preferred_element_type=F32)


def split(v):
    hi = v.astype(BF16)
    return hi, (v - hi.astype(F32)).astype(BF16)


def filter_tables(height, width):
    m = np.arange(height)
    ang = 2.0 * np.pi * (np.outer(m, m) % height) / height
    had = (np.cos(ang) + np.sin(ang)) / np.sqrt(height)
    hi = had.astype(jnp.bfloat16)
    lo = (had - hi.astype(np.float64)).astype(jnp.bfloat16)
    beta = 1.0 + STRENGTH * (2.0 - 2.0 * np.cos(2.0 * np.pi * m / height)) + 2.0 * STRENGTH
    half = beta / (2.0 * STRENGTH)
    root = half - np.sqrt(half * half - 1.0)
    scale = root / STRENGTH / (1.0 - root**width) ** 2
    wide = np.ones((1, 128))
    return (
        hi,
        lo,
        (root[:, None] * wide).astype(np.float32),
        (scale[:, None] * wide).astype(np.float32),
    )


def filter_kernel(img, hi_ref, lo_ref, root_ref, scale_ref, out, mid):
    height, width = img.shape
    chunk = 512
    h_hi = hi_ref[...]
    h_lo = lo_ref[...]

    def apply(v):
        v_hi, v_lo = split(v)
        return dot(h_hi, v_hi) + (dot(h_hi, v_lo) + dot(h_lo, v_hi))

    @pl.loop(0, width // chunk)
    def _(c):
        cols = pl.ds(pl.multiple_of(c * chunk, chunk), chunk)
        mid[:, cols] = apply(1.0 - img[:, cols])

    @pl.loop(0, height // 8)
    def _(g):
        rows = pl.ds(pl.multiple_of(g * 8, 8), 8)
        root = root_ref[rows, :]
        v = mid[rows, :]
        for back in (False, True):
            power = root
            step = 1
            while step < width:
                wide = jnp.concatenate([power] * (width // 128), axis=1)
                v = v + wide * pltpu.roll(v, width - step if back else step, 1)
                power = power * power
                step *= 2
        mid[rows, :] = v * jnp.concatenate([scale_ref[rows, :]] * (width // 128), axis=1)

    @pl.loop(0, width // chunk)
    def _(c):
        cols = pl.ds(pl.multiple_of(c * chunk, chunk), chunk)
        out[:, cols] = -jnp.log(1.0 - apply(mid[:, cols]))


def paganin(images):
    height, width = images.shape
    tables = filter_tables(height, width)
    return pl.pallas_call(
        filter_kernel,
        out_shape=jax.ShapeDtypeStruct(images.shape, F32),
        in_specs=[pl.BlockSpec(memory_space=pltpu.VMEM)] * 5,
        out_specs=pl.BlockSpec(memory_space=pltpu.VMEM),
        scratch_shapes=[pltpu.VMEM((height, width), F32)],
        compiler_params=pltpu.CompilerParams(vmem_limit_bytes=40 << 20),
        name="paganin_filter",
    )(images, *[jnp.asarray(t) for t in tables])


def sirt_kernel(
    dims,
    starts,
    offs,
    cs,
    ysend,
    x0,
    res,
    rec,
    w_hi,
    w_lo,
    xb,
    pad,
    xg,
    xh,
    zs0,
    zr0,
    zs1,
    zr1,
    dg,
    dh,
    dr,
    tile,
    th,
    tl,
    pv0,
    pr0,
    pv1,
    pr1,
    ymid,
    yt,
    weight,
    yown,
    rmid,
    s_mid,
    r_mid,
    s_left,
    r_left,
    s_right,
    r_right,
    s_x,
    r_x,
    s_z,
    r_z,
    s_loc,
):
    ns, nz, nx = dims
    slots = 4
    np_group = slots * nx
    na = ns * nz
    quads = ns // 4
    right0 = MID0 + MID
    rightn = BAND - right0
    slab = lax.axis_index("slab")
    ray = lax.axis_index("ray")
    z = ray // nx
    x = lax.rem(ray, nx)

    def at_slab(t):
        return {"slab": lax.rem(slab + t, ns), "ray": ray}

    def at_z(t):
        return {"slab": slab, "ray": lax.rem(z + t, nz) * nx + x}

    def at_x(t):
        return {"slab": slab, "ray": z * nx + lax.rem(x + t, nx)}

    barrier = pltpu.get_barrier_semaphore()
    for t in range(1, nx):
        pl.semaphore_signal(barrier, inc=1, device_id=at_x(t), device_id_type=MESH)
    for t in range(1, nz):
        pl.semaphore_signal(barrier, inc=1, device_id=at_z(t), device_id_type=MESH)
    for t in range(1, ns):
        pl.semaphore_signal(barrier, inc=1, device_id=at_slab(t), device_id_type=MESH)
    pl.semaphore_wait(barrier, nx + nz + ns - 3)

    def send(src, dst, ssem, rsem, device):
        return pltpu.make_async_remote_copy(
            src_ref=src, dst_ref=dst, send_sem=ssem, recv_sem=rsem, device_id=device, device_id_type=MESH
        )

    x_out = [
        send(x0, xg.at[x], s_x.at[0, t - 1], r_x.at[0, t - 1], at_x(t)) for t in range(1, nx)
    ]
    for c in x_out:
        c.start()
    y_mid, y_side = [], []
    for t in range(1, ns):
        to = lax.rem(slab + t, ns)
        y_mid.append(
            send(
                ysend.at[to, :, pl.ds(MID0, MID)], ymid.at[slab], s_mid.at[t - 1], r_mid.at[t - 1], at_slab(t)
            )
        )
        y_side.append(
            send(
                ysend.at[to, :, pl.ds(0, MID0)],
                res.at[slab, :, pl.ds(0, MID0)],
                s_left.at[t - 1],
                r_left.at[t - 1],
                at_slab(t),
            )
        )
        y_side.append(
            send(
                ysend.at[to, :, pl.ds(right0, rightn)],
                res.at[slab, :, pl.ds(right0, rightn)],
                s_right.at[t - 1],
                r_right.at[t - 1],
                at_slab(t),
            )
        )
    for c in y_mid + y_side:
        c.start()
    own_in = pltpu.make_async_copy(ysend.at[slab], yown, s_loc.at[0])
    own_in.start()

    vox = lax.broadcasted_iota(jnp.int32, (1, 256), 1)
    dx = (vox // 16).astype(F32) - 7.5
    dy = lax.rem(vox, 16).astype(F32) - 7.5
    lane_ray = lax.broadcasted_iota(jnp.int32, (TR, 256), 0).astype(F32)

    @pl.loop(0, na)
    def _(a):
        base = lane_ray - (dx * cs[a] + dy * cs[na + a])
        rows = pl.ds(pl.multiple_of(a * TR, TR), TR)

        @pl.loop(0, np_group)
        def _(p):
            hat = jnp.maximum(0.0, 1.0 - jnp.abs(base + offs[p * na + a]))
            hi, lo = split(hat)
            w_hi[p, rows, :] = hi
            w_lo[p, rows, :] = lo

    @pl.loop(0, ns)
    def _(a):
        for p in range(np_group):
            pad[a, pl.ds(p * STRIDE // 8, LEAD // 8)] = jnp.zeros((LEAD // 8, 8, 128), F32)
        pad[a, pl.ds(np_group * STRIDE // 8, LEAD // 8)] = jnp.zeros((LEAD // 8, 8, 128), F32)

    @pl.loop(0, np_group)
    def _(p):
        xb[p, 64:96, :] = jnp.ones((32, 256), BF16)
        xb[p, 96:128, :] = jnp.zeros((32, 256), BF16)

    lane = lax.broadcasted_iota(jnp.int32, (1, 128), 1) // 32

    def load_volume(source):
        for q in range(nx):
            for s in range(slots):
                hi, lo = split(source[q, :, pl.ds(s * 256, 256)])
                xb[q * slots + s, 0:32, :] = hi
                xb[q * slots + s, 32:64, :] = lo

    def forward(zs, zr, phase):
        with_sums = phase == 0

        @pl.loop(0, nz)
        def _(t):
            o = lax.rem(z + 1 + t, nz)
            rows = pl.ds(pl.multiple_of(o * (ns * TR), ns * TR), ns * TR)

            @pl.loop(0, np_group)
            def _(p):
                part = dot_nt(w_hi[p, rows, :], xb[p]) + dot_nt(w_lo[p, rows, :], xb[p])
                at = pl.ds(p * (STRIDE // 8) + LEAD // 8, TR // 8)
                for a in range(ns):
                    pad[a, at] = part[a * TR : (a + 1) * TR].reshape(TR // 8, 8, 128)

            @pl.loop(0, quads)
            def _(g):
                packed = jnp.zeros((RAYS, 128), F32)
                sums = jnp.zeros((RAYS, 128), F32)
                for i in range(4):
                    a = g * 4 + i
                    acc = jnp.zeros((RAYS, 128), F32)
                    for p in range(np_group):
                        first = (p * STRIDE + LEAD) // 8 - starts[p * na + o * ns + a]
                        acc = acc + pad[a, pl.ds(first, RAYS // 8)].reshape(RAYS, 128)
                    both = acc + pltpu.roll(acc, 96, 1)
                    packed = jnp.where(lane == i, pltpu.roll(both, 32 * i, 1) if i else both, packed)
                    if with_sums:
                        sums = jnp.where(
                            lane == i, pltpu.roll(acc, (64 + 32 * i) % 128, 1) if i != 2 else acc, sums
                        )
                zs[t, g] = packed
                if with_sums:
                    zs[t, quads + g] = sums

            @pl.when(t < nz - 1)
            def _():
                send(zs.at[t], zr.at[t], s_z.at[phase, t], r_z.at[phase, t], at_z(1 + t)).start()

    def end_forward(zs, zr, phase):
        for t in range(nz - 1):
            c = send(zs.at[t], zr.at[t], s_z.at[phase, t], r_z.at[phase, t], at_z(1 + t))
            c.wait_send()
            c.wait_recv()

    def total_rays(zs, zr, index):
        v = zs[nz - 1, index]
        for t in range(nz - 1):
            v = v + zr[t, index]
        return v * (1.0 / ROI)

    def spread(buf, phase):
        out = [
            send(buf.at[z], buf.at[z], s_z.at[phase, t - 1], r_z.at[phase, t - 1], at_z(t))
            for t in range(1, nz)
        ]
        for c in out:
            c.start()
        return out

    def backward(buf, pv, pr, phase):
        @pl.loop(0, nz)
        def _(o):
            for g in range(quads):
                v = buf[o, g]
                for i in range(4):
                    m = jnp.where(lane == i, v, 0.0)
                    m = m + pltpu.roll(m, 32, 1)
                    m = m + pltpu.roll(m, 64, 1)
                    dr[o * ns + g * 4 + i] = m.reshape(RAYS // 8, 8, 128)

        @pl.loop(0, nx)
        def _(t):
            q = lax.rem(x + 1 + t, nx)

            @pl.loop(0, na // 4)
            def _(b):
                for j in range(4):
                    a = b * 4 + j
                    out = None
                    for s in range(slots):
                        first = starts[(q * slots + s) * na + a]
                        v = dr[a, pl.ds(first, TR // 8)].reshape(TR, 128)
                        out = v if s == 0 else jnp.where(lane == s, v, out)
                    tile[j * TR : (j + 1) * TR, :] = out
                hi, lo = split(jnp.transpose(tile[...]))
                cols = pl.ds(pl.multiple_of(b * 128, 128), 128)
                th[:, cols] = hi
                tl[:, cols] = lo

            for s in range(slots):
                p = q * slots + s
                hi = th[s * 32 : (s + 1) * 32, :]
                lo = tl[s * 32 : (s + 1) * 32, :]
                pv[t, :, s * 256 : (s + 1) * 256] = dot(hi, w_hi[p]) + (dot(lo, w_hi[p]) + dot(hi, w_lo[p]))

            @pl.when(t < nx - 1)
            def _():
                send(pv.at[t], pr.at[t], s_x.at[phase, t], r_x.at[phase, t], at_x(1 + t)).start()

        for t in range(nx - 1):
            c = send(pv.at[t], pr.at[t], s_x.at[phase, t], r_x.at[phase, t], at_x(1 + t))
            c.wait_send()
            c.wait_recv()
        v = pv[nx - 1]
        for t in range(nx - 1):
            v = v + pr[t]
        return v * (RELAX / (ns * nz * nx))

    xg[x] = x0[...]
    for c in x_out:
        c.wait()
    load_volume(xg)
    forward(zs0, zr0, 0)

    own_in.wait()
    ymid[slab] = yown[:, MID0 : MID0 + MID]
    own_out = [
        pltpu.make_async_copy(yown.at[:, pl.ds(0, MID0)], res.at[slab, :, pl.ds(0, MID0)], s_loc.at[1]),
        pltpu.make_async_copy(
            yown.at[:, pl.ds(right0, rightn)], res.at[slab, :, pl.ds(right0, rightn)], s_loc.at[2]
        ),
    ]
    for c in own_out:
        c.start()
    for c in y_mid:
        c.wait()
    for g in range(quads):
        block = ymid[g * 4 : (g + 1) * 4].reshape(128, MID)
        for h in range(MID // 128):
            yt[g, h * 128 : (h + 1) * 128, :] = jnp.transpose(block[:, h * 128 : (h + 1) * 128])
    end_forward(zs0, zr0, 0)
    for g in range(quads):
        weight[g] = 1.0 / jnp.maximum(total_rays(zs0, zr0, quads + g), ROW_FLOOR)
        dg[z, g] = (yt[g, SKIP : SKIP + RAYS, :] - total_rays(zs0, zr0, g)) * weight[g]
    d_out = spread(dg, 1)
    for c in d_out:
        c.wait()
    first = x0[...] + backward(dg, pv0, pr0, 1)
    xh[x] = first
    x_out = [
        send(xh.at[x], xh.at[x], s_x.at[2, t - 1], r_x.at[2, t - 1], at_x(t)) for t in range(1, nx)
    ]
    for c in x_out:
        c.start()
    for c in x_out:
        c.wait()
    load_volume(xh)
    forward(zs1, zr1, 2)
    end_forward(zs1, zr1, 2)
    for g in range(quads):
        diff = yt[g, SKIP : SKIP + RAYS, :] - total_rays(zs1, zr1, g)
        dh[z, g] = diff * weight[g]
        yt[g, SKIP : SKIP + RAYS, :] = diff
    d_out = spread(dh, 3)
    for g in range(quads):
        for h in range(MID // 128):
            turned = jnp.transpose(yt[g, h * 128 : (h + 1) * 128, :])
            rmid[g * 4 : (g + 1) * 4, :, h * 128 : (h + 1) * 128] = turned.reshape(4, 32, 128)
    mid_out = pltpu.make_async_copy(rmid, res.at[:, :, pl.ds(MID0, MID)], s_loc.at[3])
    mid_out.start()
    for c in d_out:
        c.wait()
    rec[...] = first + backward(dh, pv1, pr1, 3)

    mid_out.wait()
    for c in own_out + y_side:
        c.wait()


def sirt(starts, offs, cs, ysend, x0, dims):
    ns, nz, nx = dims
    np_group = 4 * nx
    na = ns * nz
    rows = na * TR
    quads = ns // 4
    dma = pltpu.SemaphoreType.DMA
    vm = pltpu.VMEM
    smem = pl.BlockSpec(memory_space=pltpu.SMEM)
    peers_z = max(nz - 1, 1)
    peers_x = max(nx - 1, 1)
    return pl.pallas_call(
        functools.partial(sirt_kernel, dims),
        out_shape=(
            jax.ShapeDtypeStruct((ns, 32, BAND), F32),
            jax.ShapeDtypeStruct((32, 1024), F32),
        ),
        in_specs=[smem, smem, smem, pl.BlockSpec(memory_space=pl.ANY), pl.BlockSpec(memory_space=pltpu.VMEM)],
        out_specs=(pl.BlockSpec(memory_space=pl.ANY), pl.BlockSpec(memory_space=pltpu.VMEM)),
        scratch_shapes=[
            vm((np_group, rows, 256), BF16),
            vm((np_group, rows, 256), BF16),
            vm((np_group, 128, 256), BF16),
            vm((ns, (np_group * STRIDE + LEAD) // 8, 8, 128), F32),
            vm((nx, 32, 1024), F32),
            vm((nx, 32, 1024), F32),
            vm((nz, 2 * quads, RAYS, 128), F32),
            vm((peers_z, 2 * quads, RAYS, 128), F32),
            vm((nz, quads, RAYS, 128), F32),
            vm((peers_z, quads, RAYS, 128), F32),
            vm((nz, quads, RAYS, 128), F32),
            vm((nz, quads, RAYS, 128), F32),
            vm((na, RAYS // 8, 8, 128), F32),
            vm((128, 128), F32),
            vm((128, rows), BF16),
            vm((128, rows), BF16),
            vm((nx, 32, 1024), F32),
            vm((peers_x, 32, 1024), F32),
            vm((nx, 32, 1024), F32),
            vm((peers_x, 32, 1024), F32),
            vm((ns, 32, MID), F32),
            vm((quads, MID, 128), F32),
            vm((quads, RAYS, 128), F32),
            vm((32, BAND), F32),
            vm((ns, 32, MID), F32),
            dma((ns - 1,)),
            dma((ns - 1,)),
            dma((ns - 1,)),
            dma((ns - 1,)),
            dma((ns - 1,)),
            dma((ns - 1,)),
            dma((4, peers_x)),
            dma((4, peers_x)),
            dma((4, peers_z)),
            dma((4, peers_z)),
            dma((4,)),
        ],
        compiler_params=pltpu.CompilerParams(
            collective_id=0, has_side_effects=True, vmem_limit_bytes=62 << 20
        ),
        name="sirt",
    )(starts, offs, cs, ysend, x0)


def tile_tables(angles, vol_list, z, x, nz, nx):
    theta = lax.dynamic_index_in_dim(angles.reshape(-1, nz, nx), x, 2, keepdims=False)
    theta = jnp.transpose(theta).reshape(-1)
    ids = lax.dynamic_slice_in_dim(vol_list, z * 4 * nx, 4 * nx)
    cosine = jnp.cos(theta)
    sine = jnp.sin(theta)
    centre_x = (ids // PGRID).astype(F32) * 16.0 + 7.5 - HALF_ROI
    centre_y = (ids % PGRID).astype(F32) * 16.0 + 7.5 - HALF_ROI
    centre = HALF_BAND + centre_x[:, None] * cosine[None, :] + centre_y[:, None] * sine[None, :]
    first = jnp.floor(centre - 11.61).astype(jnp.int32) + 1
    start = first // 8
    offs = (start * 8).astype(F32) - centre
    return (start - RAY0 // 8).reshape(-1), offs.reshape(-1), jnp.concatenate([cosine, sine])


def local(dims, intensity, angles, volume, vol_list):
    ns, nz, nx = dims
    rank = lax.axis_index("ray")
    height = intensity.shape[2]
    sino = paganin(intensity.reshape(height, BAND))
    starts, offs, cs = tile_tables(angles, vol_list, rank // nx, rank % nx, nz, nx)
    res, rec = sirt(starts, offs, cs, sino.reshape(ns, height // ns, BAND), volume.reshape(32, 1024), dims)
    return rec.reshape(volume.shape), res[:, None]


def make(mesh, dims):
    placed = (P("slab", "ray", None, None), P(), P("slab", "ray", None), P())
    return jax.shard_map(
        functools.partial(local, dims),
        mesh=mesh,
        in_specs=placed,
        out_specs=(P("slab", "ray", None), P(None, "ray", "slab", None)),
        check_vma=False,
    )


def solution(mesh):
    return make(mesh, (mesh.shape["slab"], 4, mesh.shape["ray"] // 4))
```

time: 751 us -> 180 us (0.24)
  other arithmetic: 241 us -> 2.62 us
  local copies, waits for them, and re-layouts: 197 us -> 13.9 us
  Pallas kernels: 0 us -> 162 us
  matrix products: 149 us -> 0 us
  waiting for transfers between devices: 77.2 us -> 0 us
  blocking collectives: 31.6 us -> 0 us
  starting transfers between devices: 27.9 us -> 0 us
  between operations: 22.4 us -> 0.7 us
    scatter-add x2 -> x0, other arithmetic: 183 us -> none  [place_windows(): return empty.at[:, flat_index].add(tiles.reshape(num_rows, -1))]
    pallas_call x0 -> x2, Pallas kernels: none -> 162 us  [the longest x1 124 us: sirt(): pl.pallas_call(functools.partial(sirt_kernel, dims), out_shape=(jax.Shape...]
    dot_general x44 -> x0, matrix products: 149 us -> none  [the longest x8 36.1 us: rows_outer(): return jnp.einsum('kn,anmc->akmc', table, values, precision=highest)]
    gather x2 -> x0, local copies, waits for them, and re-layouts: 116 us -> none  [take_windows(): values[:, flat_index]]
    all_to_all x5 -> x0, waiting for transfers between devices: 77.2 us -> none  [the longest x2 45.4 us: backward(): lax.all_to_all(windows, 'ray', split_axis=1, concat_axis=2, tiled=True)]
    all_to_all x1 -> x0, blocking collectives: 31.6 us -> none  [forward(): lax.all_to_all(stacked, 'ray', split_axis=2, concat_axis=1, tiled=True)]
    another operation x16 -> x0, local copies, waits for them, and re-layouts: 28.4 us -> none  [the longest x2 12.5 us: backward(): take_windows(scaled, starts)]
    all_to_all x5 -> x0, starting transfers between devices: 27.9 us -> none  [the longest x1 8.21 us: forward(): lax.all_to_all(sum_rows, 'ray', split_axis=2, concat_axis=1, tiled=True)]
  transfers between devices with their start and end apart: 5 -> 0, of which waited for: 4 -> 0; matrix products, arithmetic and copies ran while one was open for 21% -> 0% of each run, Pallas kernels for 0% -> 0%
where the time goes in v1:
time: 180 us; the launch traced here: 179 us
  Pallas kernels  162 us (90%)
  local copies, waits for them, and re-layouts  13.9 us (8%)
  other arithmetic  2.62 us (1%)
    pallas_call x1, Pallas kernels, sirt(): pl.pallas_call(functools.partial(sirt_kernel, dims), out_shape=(jax.Shape...  124 us
    pallas_call x1, Pallas kernels, paganin(): pl.pallas_call(filter_kernel, out_shape=jax.ShapeDtypeStruct(images.shape...  38 us
    unnamed x15, local copies, waits for them, and re-layouts  12 us

profile of v1, /device:TPU:0, one launch (start us, length us, event | category | flops | bytes accessed | tf_op | source)
XLA Modules:
  0.0 178.9 jit_solution(6362100416487642650)
XLA Ops:
  0.7 0.7 multiply_add_fusion.1
  1.4 0.8 copy.10
  2.2 0.1 dynamic-slice_cosine_fusion
  2.2 0.1 cos.19
  2.3 0.1 sin.19
  2.4 0.6 pad_maximum_fusion.cs
  3.0 0.1 multiply_add_fusion
  3.1 0.1 add.67
  3.2 0.6 convert_subtract_fusion.offs
  3.8 0.6 broadcast_add_fusion.starts
  4.4 1.6 copy.12
  6.0 0.0 copy-start.1
  6.0 1.6 copy-done.1
  7.5 0.0 copy-start.2
  7.6 0.9 copy-done.2
  8.5 0.0 copy-start.3
  8.5 0.9 copy-done.3
  9.4 0.0 copy-start.4
  9.4 0.9 copy-done.4
  10.3 0.0 copy-start.5
  10.3 0.9 copy-done.5
  11.2 38.0 %paganin_filter.1 = f32[256,2048]{1,0:T(8,128)S(1)} custom-call(f32[256,2048]{1,0:T(8,128)S(1)} %bitcast.15, bf16[256,256]{1,0:T(8,128)(2,1)S(1)} %copy-done.5, bf16[256,256]{1,0:T(8,128)(2,1)S(1)} %copy-done.4, f32[256,128]{1,0:T(8,128)S(1)} %copy-done.3, f32[256,128]{1,0:T(8,128)S(1)} %copy-done.2), custom_call_target="tpu_custom_call" | custom-call | tf_op jit(solution)/shard_map/paganin_filter/pallas_call | solution.py:104
  49.2 0.0 copy-start
  49.2 1.3 copy-done
  50.5 123.6 %sirt.1 = (f32[8,32,2048]{2,1,0:T(8,128)}, f32[32,1024]{1,0:T(8,128)}) custom-call(s32[512]{0:T(512)} %broadcast_add_fusion.starts, f32[512]{0:T(512)} %convert_subtract_fusion.offs, f32[64]{0:T(128)} %pad_maximum_fusion.cs, f32[8,32,2048]{2,1,0:T(8,128)} %bitcast.14, f32[32,1024]{1,0:T(8,128)} %bitcast.17), custom_call_target="tpu_custom_call" | custom-call | tf_op jit(solution)/shard_map/sirt/pallas_call | solution.py:450
  174.1 1.6 reshape.55
  175.7 3.1 %copy.14 = f32[8,1,32,2048]{3,2,1,0:T(8,128)} copy(f32[8,1,32,2048]{3,2,1,0:T(8,128)} %bitcast.16) | data formatting | bytes 4194304
  (1 shorter events, 0.0 us)
Async XLA Ops:
  6.0 1.6 copy-start.1
  7.5 0.9 copy-start.2
  8.5 0.9 copy-start.3
  9.4 0.9 copy-start.4
  10.3 0.9 copy-start.5
  49.2 1.3 copy-start

commit v2 on v1

--- a/solution.py
+++ b/solution.py
@@ -28,6 +28,7 @@
 LEAD = RAYS - TR
 F32 = jnp.float32
 BF16 = jnp.bfloat16
+HALO = 64
 
 
 def dot(a, b):
@@ -53,63 +54,75 @@
     half = beta / (2.0 * STRENGTH)
     root = half - np.sqrt(half * half - 1.0)
     scale = root / STRENGTH / (1.0 - root**width) ** 2
-    wide = np.ones((1, 128))
-    return (
-        hi,
-        lo,
-        (root[:, None] * wide).astype(np.float32),
-        (scale[:, None] * wide).astype(np.float32),
-    )
-
-
-def filter_kernel(img, hi_ref, lo_ref, root_ref, scale_ref, out, mid):
+    steps = int(np.log2(width))
+    table = np.zeros((16, height))
+    power = root
+    for k in range(steps):
+        table[k] = power / (1.0 + power * power)
+        scale = scale * (1.0 + power * power)
+        power = power * power
+    table[15] = scale
+    return hi, lo, table.astype(np.float32)
+
+
+def filter_forward(img, h_hi, h_lo, table, ping, pong):
     height, width = img.shape
-    chunk = 512
-    h_hi = hi_ref[...]
-    h_lo = lo_ref[...]
-
-    def apply(v):
-        v_hi, v_lo = split(v)
-        return dot(h_hi, v_hi) + (dot(h_hi, v_lo) + dot(h_lo, v_hi))
+    chunk = 256
+    halves = height // 128
 
     @pl.loop(0, width // chunk)
     def _(c):
         cols = pl.ds(pl.multiple_of(c * chunk, chunk), chunk)
-        mid[:, cols] = apply(1.0 - img[:, cols])
-
-    @pl.loop(0, height // 8)
-    def _(g):
-        rows = pl.ds(pl.multiple_of(g * 8, 8), 8)
-        root = root_ref[rows, :]
-        v = mid[rows, :]
-        for back in (False, True):
-            power = root
-            step = 1
-            while step < width:
-                wide = jnp.concatenate([power] * (width // 128), axis=1)
-                v = v + wide * pltpu.roll(v, width - step if back else step, 1)
-                power = power * power
-                step *= 2
-        mid[rows, :] = v * jnp.concatenate([scale_ref[rows, :]] * (width // 128), axis=1)
-
-    @pl.loop(0, width // chunk)
-    def _(c):
-        cols = pl.ds(pl.multiple_of(c * chunk, chunk), chunk)
-        out[:, cols] = -jnp.log(1.0 - apply(mid[:, cols]))
-
-
-def paganin(images):
-    height, width = images.shape
-    tables = filter_tables(height, width)
-    return pl.pallas_call(
-        filter_kernel,
-        out_shape=jax.ShapeDtypeStruct(images.shape, F32),
-        in_specs=[pl.BlockSpec(memory_space=pltpu.VMEM)] * 5,
-        out_specs=pl.BlockSpec(memory_space=pltpu.VMEM),
-        scratch_shapes=[pltpu.VMEM((height, width), F32)],
-        compiler_params=pltpu.CompilerParams(vmem_limit_bytes=40 << 20),
-        name="paganin_filter",
-    )(images, *[jnp.asarray(t) for t in tables])
+        rows = pl.ds(pl.multiple_of(HALO + c * chunk, 8), chunk)
+        v_hi, v_lo = split(jnp.transpose(1.0 - img[:, cols]))
+        v = dot(v_hi, h_hi[...]) + (dot(v_lo, h_hi[...]) + dot(v_hi, h_lo[...]))
+        for h in range(halves):
+            ping[h, rows, :] = v[:, h * 128 : (h + 1) * 128]
+
+    def row(k, h):
+        return jnp.broadcast_to(table[k : k + 1, h * 128 : (h + 1) * 128], (8, 128))
+
+    source, target = ping, pong
+    step, k = 1, 0
+    while step <= HALO:
+        for h in range(halves):
+            source[h, 0:HALO, :] = source[h, width : width + HALO, :]
+            source[h, width + HALO : width + 2 * HALO, :] = source[h, HALO : 2 * HALO, :]
+            rate = row(k, h)
+
+            @pl.loop(0, width // 128)
+            def _(b, h=h, step=step, source=source, target=target, rate=rate):
+                for i in range(16):
+                    at = b * 128 + HALO + 8 * i
+                    here = source[h, pl.ds(at, 8), :]
+                    near = source[h, pl.ds(at - step, 8), :] + source[h, pl.ds(at + step, 8), :]
+                    target[h, pl.ds(at, 8), :] = here + rate * near
+
+        source, target = target, source
+        step *= 2
+        k += 1
+
+    for h in range(halves):
+        rates = [row(j, h) for j in range(k, k + 4)]
+        scale = row(15, h)
+
+        @pl.loop(0, 16)
+        def _(i, h=h, rates=rates, scale=scale):
+            v = [source[h, pl.ds(HALO + b * 128 + 8 * i, 8), :] for b in range(16)]
+            for j, rate in zip((1, 2, 4, 8), rates):
+                v = [v[b] + rate * (v[b - j] + v[(b + j) % 16]) for b in range(16)]
+            for b in range(16):
+                target[h, pl.ds(HALO + b * 128 + 8 * i, 8), :] = v[b] * scale
+
+    return target
+
+
+def filter_back(modes, h_hi, h_lo, out, first, count):
+    rows = pl.ds(HALO + first, count)
+    v = jnp.concatenate([modes[h, rows, :] for h in range(out.shape[0] // 128)], axis=1)
+    v_hi, v_lo = split(v)
+    v = dot_nt(h_hi[...], v_hi) + (dot_nt(h_hi[...], v_lo) + dot_nt(h_lo[...], v_hi))
+    out[:, pl.ds(first, count)] = -jnp.log(1.0 - v)
 
 
 def sirt_kernel(
@@ -117,10 +130,25 @@
     starts,
     offs,
     cs,
-    ysend,
+    image,
+    h_hi_in,
+    h_lo_in,
+    table_in,
     x0,
     res,
     rec,
+    img,
+    ping,
+    pong,
+    h_hi,
+    h_lo,
+    table,
+    parts_hi,
+    parts_lo,
+    pick,
+    sums_pick,
+    copy_out,
+    copy_sum,
     w_hi,
     w_lo,
     xb,
@@ -136,7 +164,6 @@
     dr,
     tile,
     th,
-    tl,
     pv0,
     pr0,
     pv1,
@@ -144,7 +171,6 @@
     ymid,
     yt,
     weight,
-    yown,
     rmid,
     s_mid,
     r_mid,
@@ -179,6 +205,14 @@
     def at_x(t):
         return {"slab": slab, "ray": z * nx + lax.rem(x + t, nx)}
 
+    loads = [
+        pltpu.make_async_copy(image, img, s_loc.at[0]),
+        pltpu.make_async_copy(h_hi_in, h_hi, s_loc.at[4]),
+        pltpu.make_async_copy(h_lo_in, h_lo, s_loc.at[5]),
+        pltpu.make_async_copy(table_in, table, s_loc.at[6]),
+    ]
+    for c in loads:
+        c.start()
     barrier = pltpu.get_barrier_semaphore()
     for t in range(1, nx):
         pl.semaphore_signal(barrier, inc=1, device_id=at_x(t), device_id_type=MESH)
@@ -199,16 +233,17 @@
     for c in x_out:
         c.start()
     y_mid, y_side = [], []
+    own_rows = pl.ds(pl.multiple_of(slab * 32, 32), 32)
     for t in range(1, ns):
-        to = lax.rem(slab + t, ns)
+        to = pl.ds(pl.multiple_of(lax.rem(slab + t, ns) * 32, 32), 32)
         y_mid.append(
             send(
-                ysend.at[to, :, pl.ds(MID0, MID)], ymid.at[slab], s_mid.at[t - 1], r_mid.at[t - 1], at_slab(t)
+                img.at[to, pl.ds(MID0, MID)], ymid.at[slab], s_mid.at[t - 1], r_mid.at[t - 1], at_slab(t)
             )
         )
         y_side.append(
             send(
-                ysend.at[to, :, pl.ds(0, MID0)],
+                img.at[to, pl.ds(0, MID0)],
                 res.at[slab, :, pl.ds(0, MID0)],
                 s_left.at[t - 1],
                 r_left.at[t - 1],
@@ -217,17 +252,13 @@
         )
         y_side.append(
             send(
-                ysend.at[to, :, pl.ds(right0, rightn)],
+                img.at[to, pl.ds(right0, rightn)],
                 res.at[slab, :, pl.ds(right0, rightn)],
                 s_right.at[t - 1],
                 r_right.at[t - 1],
                 at_slab(t),
             )
         )
-    for c in y_mid + y_side:
-        c.start()
-    own_in = pltpu.make_async_copy(ysend.at[slab], yown, s_loc.at[0])
-    own_in.start()
 
     vox = lax.broadcasted_iota(jnp.int32, (1, 256), 1)
     dx = (vox // 16).astype(F32) - 7.5
@@ -259,6 +290,19 @@
 
     lane = lax.broadcasted_iota(jnp.int32, (1, 128), 1) // 32
 
+    def one_hot(shape, test):
+        r = lax.broadcasted_iota(jnp.int32, shape, 0)
+        c = lax.broadcasted_iota(jnp.int32, shape, 1)
+        return jnp.where(test(r, c), 1.0, 0.0).astype(BF16)
+
+    pick[...] = one_hot(
+        (512, 128), lambda r, c: (r % 128 < 64) & (r % 32 == c % 32) & (r // 128 == c // 32)
+    )
+    for g in range(quads):
+        sums_pick[g] = one_hot((512, 128), lambda r, c, g=g: (r % 128 == 64) & (g * 4 + r // 128 == c // 16))
+        copy_sum[g] = one_hot((128, 128), lambda r, c, g=g: r == (g * 4 + c // 32) * 16)
+    copy_out[...] = one_hot((128, 512), lambda r, c: (r // 32 == c // 128) & (r % 32 == c % 32))
+
     def load_volume(source):
         for q in range(nx):
             for s in range(slots):
@@ -274,7 +318,7 @@
             o = lax.rem(z + 1 + t, nz)
             rows = pl.ds(pl.multiple_of(o * (ns * TR), ns * TR), ns * TR)
 
-            @pl.loop(0, np_group)
+            @pl.loop(0, np_group, unroll=8)
             def _(p):
                 part = dot_nt(w_hi[p, rows, :], xb[p]) + dot_nt(w_lo[p, rows, :], xb[p])
                 at = pl.ds(p * (STRIDE // 8) + LEAD // 8, TR // 8)
@@ -283,23 +327,19 @@
 
             @pl.loop(0, quads)
             def _(g):
-                packed = jnp.zeros((RAYS, 128), F32)
-                sums = jnp.zeros((RAYS, 128), F32)
                 for i in range(4):
                     a = g * 4 + i
                     acc = jnp.zeros((RAYS, 128), F32)
                     for p in range(np_group):
                         first = (p * STRIDE + LEAD) // 8 - starts[p * na + o * ns + a]
                         acc = acc + pad[a, pl.ds(first, RAYS // 8)].reshape(RAYS, 128)
-                    both = acc + pltpu.roll(acc, 96, 1)
-                    packed = jnp.where(lane == i, pltpu.roll(both, 32 * i, 1) if i else both, packed)
-                    if with_sums:
-                        sums = jnp.where(
-                            lane == i, pltpu.roll(acc, (64 + 32 * i) % 128, 1) if i != 2 else acc, sums
-                        )
-                zs[t, g] = packed
+                    hi, lo = split(acc)
+                    parts_hi[:, i * 128 : (i + 1) * 128] = hi
+                    parts_lo[:, i * 128 : (i + 1) * 128] = lo
+                zs[t, g] = dot(parts_hi[...], pick[...]) + dot(parts_lo[...], pick[...])
                 if with_sums:
-                    zs[t, quads + g] = sums
+                    part = dot(parts_hi[...], sums_pick[g]) + dot(parts_lo[...], sums_pick[g])
+                    zs[t, quads] = jnp.where(g == 0, part, part + zs[t, quads])
 
             @pl.when(t < nz - 1)
             def _():
@@ -327,44 +367,51 @@
         return out
 
     def backward(buf, pv, pr, phase):
+        pv[...] = jnp.zeros_like(pv)
+
         @pl.loop(0, nz)
-        def _(o):
+        def _(t):
+            off = t + t // 2 - 2 * (t // 3)
+            o = lax.rem(z + nz - off, nz)
+
+            @pl.when(t > 0)
+            def _():
+                send(buf.at[o], buf.at[o], s_z.at[phase, off - 1], r_z.at[phase, off - 1], at_z(1)).wait_recv()
+
             for g in range(quads):
-                v = buf[o, g]
+                hi, lo = split(buf[o, g])
+                wide = dot(hi, copy_out[...]) + dot(lo, copy_out[...])
                 for i in range(4):
-                    m = jnp.where(lane == i, v, 0.0)
-                    m = m + pltpu.roll(m, 32, 1)
-                    m = m + pltpu.roll(m, 64, 1)
-                    dr[o * ns + g * 4 + i] = m.reshape(RAYS // 8, 8, 128)
-
-        @pl.loop(0, nx)
-        def _(t):
-            q = lax.rem(x + 1 + t, nx)
-
-            @pl.loop(0, na // 4)
-            def _(b):
-                for j in range(4):
-                    a = b * 4 + j
-                    out = None
+                    dr[g * 4 + i] = wide[:, i * 128 : (i + 1) * 128].reshape(RAYS // 8, 8, 128)
+
+            rows = pl.ds(pl.multiple_of(o * (ns * TR), ns * TR), ns * TR)
+
+            @pl.loop(0, nx)
+            def _(u):
+                q = lax.rem(x + 1 + u, nx)
+                for g in range(quads):
+                    for j in range(4):
+                        a = g * 4 + j
+                        out = None
+                        for s in range(slots):
+                            first = starts[(q * slots + s) * na + o * ns + a]
+                            v = dr[a, pl.ds(first, TR // 8)].reshape(TR, 128)
+                            out = v if s == 0 else jnp.where(lane == s, v, out)
+                        tile[j * TR : (j + 1) * TR, :] = out
+                    hi, lo = split(jnp.transpose(tile[...]))
                     for s in range(slots):
-                        first = starts[(q * slots + s) * na + a]
-                        v = dr[a, pl.ds(first, TR // 8)].reshape(TR, 128)
-                        out = v if s == 0 else jnp.where(lane == s, v, out)
-                    tile[j * TR : (j + 1) * TR, :] = out
-                hi, lo = split(jnp.transpose(tile[...]))
-                cols = pl.ds(pl.multiple_of(b * 128, 128), 128)
-                th[:, cols] = hi
-                tl[:, cols] = lo
-
-            for s in range(slots):
-                p = q * slots + s
-                hi = th[s * 32 : (s + 1) * 32, :]
-                lo = tl[s * 32 : (s + 1) * 32, :]
-                pv[t, :, s * 256 : (s + 1) * 256] = dot(hi, w_hi[p]) + (dot(lo, w_hi[p]) + dot(hi, w_lo[p]))
-
-            @pl.when(t < nx - 1)
-            def _():
-                send(pv.at[t], pr.at[t], s_x.at[phase, t], r_x.at[phase, t], at_x(1 + t)).start()
+                        th[s, 0:32, g * 128 : (g + 1) * 128] = hi[s * 32 : (s + 1) * 32]
+                        th[s, 32:64, g * 128 : (g + 1) * 128] = lo[s * 32 : (s + 1) * 32]
+                for s in range(slots):
+                    p = q * slots + s
+                    both = dot(th[s], w_hi[p, rows, :])
+                    low = dot(th[s, 0:32], w_lo[p, rows, :])
+                    cols = slice(s * 256, (s + 1) * 256)
+                    pv[u, :, cols] = pv[u, :, cols] + (both[:32] + (both[32:] + low))
+
+                @pl.when((t == nz - 1) & (u < nx - 1))
+                def _():
+                    send(pv.at[u], pr.at[u], s_x.at[phase, u], r_x.at[phase, u], at_x(1 + u)).start()
 
         for t in range(nx - 1):
             c = send(pv.at[t], pr.at[t], s_x.at[phase, t], r_x.at[phase, t], at_x(1 + t))
@@ -375,18 +422,33 @@
             v = v + pr[t]
         return v * (RELAX / (ns * nz * nx))
 
+    for c in loads:
+        c.wait()
+    modes = filter_forward(img, h_hi, h_lo, table, ping, pong)
+
     xg[x] = x0[...]
     for c in x_out:
         c.wait()
     load_volume(xg)
     forward(zs0, zr0, 0)
 
-    own_in.wait()
-    ymid[slab] = yown[:, MID0 : MID0 + MID]
+    filter_back(modes, h_hi, h_lo, img, MID0, MID)
+    for c in y_mid:
+        c.start()
+    for base in (0, right0):
+
+        @pl.loop(0, 3)
+        def _(i, base=base):
+            filter_back(modes, h_hi, h_lo, img, pl.multiple_of(base + i * 256, 128), 256)
+
+        filter_back(modes, h_hi, h_lo, img, base + 768, 128)
+    for c in y_side:
+        c.start()
+    ymid[slab] = img[own_rows, MID0 : MID0 + MID]
     own_out = [
-        pltpu.make_async_copy(yown.at[:, pl.ds(0, MID0)], res.at[slab, :, pl.ds(0, MID0)], s_loc.at[1]),
+        pltpu.make_async_copy(img.at[own_rows, pl.ds(0, MID0)], res.at[slab, :, pl.ds(0, MID0)], s_loc.at[1]),
         pltpu.make_async_copy(
-            yown.at[:, pl.ds(right0, rightn)], res.at[slab, :, pl.ds(right0, rightn)], s_loc.at[2]
+            img.at[own_rows, pl.ds(right0, rightn)], res.at[slab, :, pl.ds(right0, rightn)], s_loc.at[2]
         ),
     ]
     for c in own_out:
@@ -398,13 +460,15 @@
         for h in range(MID // 128):
             yt[g, h * 128 : (h + 1) * 128, :] = jnp.transpose(block[:, h * 128 : (h + 1) * 128])
     end_forward(zs0, zr0, 0)
+    inverse = 1.0 / jnp.maximum(total_rays(zs0, zr0, quads), ROW_FLOOR)
+    inv_hi, inv_lo = split(inverse)
     for g in range(quads):
-        weight[g] = 1.0 / jnp.maximum(total_rays(zs0, zr0, quads + g), ROW_FLOOR)
+        weight[g] = dot(inv_hi, copy_sum[g]) + dot(inv_lo, copy_sum[g])
         dg[z, g] = (yt[g, SKIP : SKIP + RAYS, :] - total_rays(zs0, zr0, g)) * weight[g]
     d_out = spread(dg, 1)
+    first = x0[...] + backward(dg, pv0, pr0, 1)
     for c in d_out:
-        c.wait()
-    first = x0[...] + backward(dg, pv0, pr0, 1)
+        c.wait_send()
     xh[x] = first
     x_out = [
         send(xh.at[x], xh.at[x], s_x.at[2, t - 1], r_x.at[2, t - 1], at_x(t)) for t in range(1, nx)
@@ -427,16 +491,19 @@
             rmid[g * 4 : (g + 1) * 4, :, h * 128 : (h + 1) * 128] = turned.reshape(4, 32, 128)
     mid_out = pltpu.make_async_copy(rmid, res.at[:, :, pl.ds(MID0, MID)], s_loc.at[3])
     mid_out.start()
+    rec[...] = first + backward(dh, pv1, pr1, 3)
     for c in d_out:
-        c.wait()
-    rec[...] = first + backward(dh, pv1, pr1, 3)
+        c.wait_send()
 
     mid_out.wait()
     for c in own_out + y_side:
         c.wait()
 
 
-def sirt(starts, offs, cs, ysend, x0, dims):
+def sirt(starts, offs, cs, image, x0, dims):
+    height, width = image.shape
+    h_hi, h_lo, table = filter_tables(height, width)
+    anywhere = pl.BlockSpec(memory_space=pl.ANY)
     ns, nz, nx = dims
     np_group = 4 * nx
     na = ns * nz
@@ -453,25 +520,36 @@
             jax.ShapeDtypeStruct((ns, 32, BAND), F32),
             jax.ShapeDtypeStruct((32, 1024), F32),
         ),
-        in_specs=[smem, smem, smem, pl.BlockSpec(memory_space=pl.ANY), pl.BlockSpec(memory_space=pltpu.VMEM)],
+        in_specs=[smem] * 3 + [anywhere] * 4 + [pl.BlockSpec(memory_space=pltpu.VMEM)],
         out_specs=(pl.BlockSpec(memory_space=pl.ANY), pl.BlockSpec(memory_space=pltpu.VMEM)),
         scratch_shapes=[
+            vm((height, width), F32),
+            vm((height // 128, width + 2 * HALO, 128), F32),
+            vm((height // 128, width + 2 * HALO, 128), F32),
+            vm(h_hi.shape, BF16),
+            vm(h_lo.shape, BF16),
+            vm(table.shape, F32),
+            vm((RAYS, 512), BF16),
+            vm((RAYS, 512), BF16),
+            vm((512, 128), BF16),
+            vm((quads, 512, 128), BF16),
+            vm((128, 512), BF16),
+            vm((quads, 128, 128), BF16),
             vm((np_group, rows, 256), BF16),
             vm((np_group, rows, 256), BF16),
             vm((np_group, 128, 256), BF16),
             vm((ns, (np_group * STRIDE + LEAD) // 8, 8, 128), F32),
             vm((nx, 32, 1024), F32),
             vm((nx, 32, 1024), F32),
-            vm((nz, 2 * quads, RAYS, 128), F32),
-            vm((peers_z, 2 * quads, RAYS, 128), F32),
+            vm((nz, quads + 1, RAYS, 128), F32),
+            vm((peers_z, quads + 1, RAYS, 128), F32),
             vm((nz, quads, RAYS, 128), F32),
             vm((peers_z, quads, RAYS, 128), F32),
             vm((nz, quads, RAYS, 128), F32),
             vm((nz, quads, RAYS, 128), F32),
-            vm((na, RAYS // 8, 8, 128), F32),
+            vm((ns, RAYS // 8, 8, 128), F32),
             vm((128, 128), F32),
-            vm((128, rows), BF16),
-            vm((128, rows), BF16),
+            vm((4, 64, ns * TR), BF16),
             vm((nx, 32, 1024), F32),
             vm((peers_x, 32, 1024), F32),
             vm((nx, 32, 1024), F32),
@@ -479,7 +557,6 @@
             vm((ns, 32, MID), F32),
             vm((quads, MID, 128), F32),
             vm((quads, RAYS, 128), F32),
-            vm((32, BAND), F32),
             vm((ns, 32, MID), F32),
             dma((ns - 1,)),
             dma((ns - 1,)),
@@ -491,13 +568,13 @@
             dma((4, peers_x)),
             dma((4, peers_z)),
             dma((4, peers_z)),
-            dma((4,)),
+            dma((8,)),
         ],
         compiler_params=pltpu.CompilerParams(
             collective_id=0, has_side_effects=True, vmem_limit_bytes=62 << 20
         ),
         name="sirt",
-    )(starts, offs, cs, ysend, x0)
+    )(starts, offs, cs, image, jnp.asarray(h_hi), jnp.asarray(h_lo), jnp.asarray(table), x0)
 
 
 def tile_tables(angles, vol_list, z, x, nz, nx):
@@ -519,9 +596,8 @@
     ns, nz, nx = dims
     rank = lax.axis_index("ray")
     height = intensity.shape[2]
-    sino = paganin(intensity.reshape(height, BAND))
     starts, offs, cs = tile_tables(angles, vol_list, rank // nx, rank % nx, nz, nx)
-    res, rec = sirt(starts, offs, cs, sino.reshape(ns, height // ns, BAND), volume.reshape(32, 1024), dims)
+    res, rec = sirt(starts, offs, cs, intensity.reshape(height, BAND), volume.reshape(32, 1024), dims)
     return rec.reshape(volume.shape), res[:, None]
 
 

time: 180 us -> 124 us (0.69)
  Pallas kernels: 162 us -> 113 us
  local copies, waits for them, and re-layouts: 13.9 us -> 7.42 us
    pallas_call x1 -> x0, Pallas kernels: 38 us -> none  [paganin(): pl.pallas_call(filter_kernel, out_shape=jax.ShapeDtypeStruct(images.shape...]
    pallas_call x1, Pallas kernels: 124 us -> 113 us  [sirt(): pl.pallas_call(functools.partial(sirt_kernel, dims), out_shape=(jax.Shape...]
    unnamed x15 -> x3, local copies, waits for them, and re-layouts: 12 us -> 5.48 us
where the time goes in v2:
time: 124 us
  Pallas kernels  113 us (91%)
  local copies, waits for them, and re-layouts  7.42 us (6%)
  other arithmetic  2.68 us (2%)
    pallas_call x1, Pallas kernels, sirt(): pl.pallas_call(functools.partial(sirt_kernel, dims), out_shape=(jax.Shape...  113 us
    unnamed x3, local copies, waits for them, and re-layouts  5.48 us

profile of v2, /device:TPU:0, one launch (start us, length us, event | category | flops | bytes accessed | tf_op | source)
XLA Modules:
  0.0 124.0 jit_solution(1007017991550739899)
XLA Ops:
  0.7 0.7 multiply_add_fusion.1
  1.4 0.8 copy.9
  2.2 0.1 dynamic-slice_cosine_fusion
  2.2 0.1 cos.19
  2.3 0.1 sin.19
  2.4 0.7 pad_maximum_fusion.cs
  3.1 0.1 multiply_add_fusion
  3.2 0.1 add.67
  3.2 0.6 convert_subtract_fusion.offs
  3.8 0.6 broadcast_add_fusion.starts
  4.4 1.6 %copy.11 = f32[4,8,4,256]{3,1,2,0:T(8,128)} copy(f32[4,8,4,256]{3,2,1,0:T(4,128)} %bitcast.16) | data formatting | bytes 262144
  6.0 113.2 %sirt.1 = (f32[8,32,2048]{2,1,0:T(8,128)}, f32[32,1024]{1,0:T(8,128)}) custom-call(s32[512]{0:T(512)} %broadcast_add_fusion.starts, f32[512]{0:T(512)} %convert_subtract_fusion.offs, f32[64]{0:T(128)} %pad_maximum_fusion.cs, f32[256,2048]{1,0:T(8,128)} %bitcast.13, bf16[256,256]{1,0:T(8,128)(2,1)} %constant.97.clone.h_hi_in, ...), custom_call_target="tpu_custom_call" | custom-call | tf_op jit(solution)/shard_map/sirt/pallas_call | solution.py:517
  119.2 1.6 %reshape.51 = f32[32,4,256]{2,1,0:T(4,128)} reshape(f32[32,1024]{1,0:T(8,128)} %get-tuple-element.4) | data formatting | bytes 262144 | tf_op jit(solution)/shard_map/reshape | solution.py:601
  120.8 3.1 %copy.13 = f32[8,1,32,2048]{3,2,1,0:T(8,128)} copy(f32[8,1,32,2048]{3,2,1,0:T(8,128)} %bitcast.14) | data formatting | bytes 4194304
  (1 shorter events, 0.0 us)

commit v3 on v2

--- a/solution.py
+++ b/solution.py
@@ -39,6 +39,10 @@
     return lax.dot_general(a, b, (((1,), (1,)), ((), ())), preferred_element_type=F32)
 
 
+def dot_tn(a, b):
+    return lax.dot_general(a, b, (((0,), (0,)), ((), ())), preferred_element_type=F32)
+
+
 def split(v):
     hi = v.astype(BF16)
     return hi, (v - hi.astype(F32)).astype(BF16)
@@ -48,8 +52,6 @@
     m = np.arange(height)
     ang = 2.0 * np.pi * (np.outer(m, m) % height) / height
     had = (np.cos(ang) + np.sin(ang)) / np.sqrt(height)
-    hi = had.astype(jnp.bfloat16)
-    lo = (had - hi.astype(np.float64)).astype(jnp.bfloat16)
     beta = 1.0 + STRENGTH * (2.0 - 2.0 * np.cos(2.0 * np.pi * m / height)) + 2.0 * STRENGTH
     half = beta / (2.0 * STRENGTH)
     root = half - np.sqrt(half * half - 1.0)
@@ -62,7 +64,7 @@
         scale = scale * (1.0 + power * power)
         power = power * power
     table[15] = scale
-    return hi, lo, table.astype(np.float32)
+    return np.concatenate([had, table]).astype(np.float32)
 
 
 def filter_forward(img, h_hi, h_lo, table, ping, pong):
@@ -131,24 +133,22 @@
     offs,
     cs,
     image,
-    h_hi_in,
-    h_lo_in,
     table_in,
-    x0,
+    volume,
     res,
     rec,
+    x0,
     img,
     ping,
     pong,
     h_hi,
     h_lo,
-    table,
     parts_hi,
     parts_lo,
     pick,
-    sums_pick,
     copy_out,
     copy_sum,
+    sums,
     w_hi,
     w_lo,
     xb,
@@ -171,7 +171,10 @@
     ymid,
     yt,
     weight,
-    rmid,
+    zsum,
+    zrsum,
+    s_sum,
+    r_sum,
     s_mid,
     r_mid,
     s_left,
@@ -206,12 +209,13 @@
         return {"slab": slab, "ray": z * nx + lax.rem(x + t, nx)}
 
     loads = [
-        pltpu.make_async_copy(image, img, s_loc.at[0]),
-        pltpu.make_async_copy(h_hi_in, h_hi, s_loc.at[4]),
-        pltpu.make_async_copy(h_lo_in, h_lo, s_loc.at[5]),
-        pltpu.make_async_copy(table_in, table, s_loc.at[6]),
+        pltpu.make_async_copy(image, img, s_loc.at[7]),
     ]
-    for c in loads:
+    x_loads = [
+        pltpu.make_async_copy(volume.at[:, s, :], x0.at[:, pl.ds(s * 256, 256)], s_loc.at[s])
+        for s in range(slots)
+    ]
+    for c in x_loads + loads:
         c.start()
     barrier = pltpu.get_barrier_semaphore()
     for t in range(1, nx):
@@ -227,6 +231,8 @@
             src_ref=src, dst_ref=dst, send_sem=ssem, recv_sem=rsem, device_id=device, device_id_type=MESH
         )
 
+    for c in x_loads:
+        c.wait()
     x_out = [
         send(x0, xg.at[x], s_x.at[0, t - 1], r_x.at[0, t - 1], at_x(t)) for t in range(1, nx)
     ]
@@ -260,6 +266,10 @@
             )
         )
 
+    height = img.shape[0]
+    h_hi[...], h_lo[...] = split(table_in[0:height, :])
+    table = table_in.at[pl.ds(height, 16), :]
+
     vox = lax.broadcasted_iota(jnp.int32, (1, 256), 1)
     dx = (vox // 16).astype(F32) - 7.5
     dy = lax.rem(vox, 16).astype(F32) - 7.5
@@ -267,12 +277,12 @@
 
     @pl.loop(0, na)
     def _(a):
-        base = lane_ray - (dx * cs[a] + dy * cs[na + a])
+        base = lane_ray - (dx * cs[0, a] + dy * cs[8, a])
         rows = pl.ds(pl.multiple_of(a * TR, TR), TR)
 
         @pl.loop(0, np_group)
         def _(p):
-            hat = jnp.maximum(0.0, 1.0 - jnp.abs(base + offs[p * na + a]))
+            hat = jnp.maximum(0.0, 1.0 - jnp.abs(base + offs[p, a]))
             hi, lo = split(hat)
             w_hi[p, rows, :] = hi
             w_lo[p, rows, :] = lo
@@ -295,12 +305,14 @@
         c = lax.broadcasted_iota(jnp.int32, shape, 1)
         return jnp.where(test(r, c), 1.0, 0.0).astype(BF16)
 
-    pick[...] = one_hot(
-        (512, 128), lambda r, c: (r % 128 < 64) & (r % 32 == c % 32) & (r // 128 == c // 32)
-    )
     for g in range(quads):
-        sums_pick[g] = one_hot((512, 128), lambda r, c, g=g: (r % 128 == 64) & (g * 4 + r // 128 == c // 16))
-        copy_sum[g] = one_hot((128, 128), lambda r, c, g=g: r == (g * 4 + c // 32) * 16)
+        pick[g, :, 0:128] = one_hot(
+            (512, 128), lambda r, c: (r % 128 < 64) & (r % 32 == c % 32) & (r // 128 == c // 32)
+        )
+        pick[g, :, 128:256] = one_hot(
+            (512, 128), lambda r, c, g=g: (r % 128 == 64) & (g * 4 + r // 128 == c)
+        )
+        copy_sum[g] = one_hot((16, 128), lambda r, c, g=g: r == g * 4 + c // 32)
     copy_out[...] = one_hot((128, 512), lambda r, c: (r // 32 == c // 128) & (r % 32 == c % 32))
 
     def load_volume(source):
@@ -331,25 +343,38 @@
                     a = g * 4 + i
                     acc = jnp.zeros((RAYS, 128), F32)
                     for p in range(np_group):
-                        first = (p * STRIDE + LEAD) // 8 - starts[p * na + o * ns + a]
+                        first = (p * STRIDE + LEAD) // 8 - starts[p, o * ns + a]
                         acc = acc + pad[a, pl.ds(first, RAYS // 8)].reshape(RAYS, 128)
                     hi, lo = split(acc)
                     parts_hi[:, i * 128 : (i + 1) * 128] = hi
                     parts_lo[:, i * 128 : (i + 1) * 128] = lo
-                zs[t, g] = dot(parts_hi[...], pick[...]) + dot(parts_lo[...], pick[...])
                 if with_sums:
-                    part = dot(parts_hi[...], sums_pick[g]) + dot(parts_lo[...], sums_pick[g])
-                    zs[t, quads] = jnp.where(g == 0, part, part + zs[t, quads])
+                    part = dot(parts_hi[...], pick[g]) + dot(parts_lo[...], pick[g])
+                    zs[t, g] = part[:, :128]
+                    sums[...] = jnp.where(g == 0, part[:, 128:], part[:, 128:] + sums[...])
+                else:
+                    zs[t, g] = dot(parts_hi[...], pick[0, :, 0:128]) + dot(parts_lo[...], pick[0, :, 0:128])
+
+            if with_sums:
+                zsum[t, :, 0:128] = jnp.transpose(sums[0:128])[0:ns]
+                zsum[t, :, 128:RAYS] = jnp.transpose(sums[128:RAYS])[0:ns]
+                zsum[t, :, RAYS:256] = jnp.ones((ns, 256 - RAYS), F32)
 
             @pl.when(t < nz - 1)
             def _():
                 send(zs.at[t], zr.at[t], s_z.at[phase, t], r_z.at[phase, t], at_z(1 + t)).start()
+                if with_sums:
+                    send(zsum.at[t], zrsum.at[t], s_sum.at[t], r_sum.at[t], at_z(1 + t)).start()
 
     def end_forward(zs, zr, phase):
         for t in range(nz - 1):
             c = send(zs.at[t], zr.at[t], s_z.at[phase, t], r_z.at[phase, t], at_z(1 + t))
             c.wait_send()
             c.wait_recv()
+            if phase == 0:
+                c = send(zsum.at[t], zrsum.at[t], s_sum.at[t], r_sum.at[t], at_z(1 + t))
+                c.wait_send()
+                c.wait_recv()
 
     def total_rays(zs, zr, index):
         v = zs[nz - 1, index]
@@ -394,7 +419,7 @@
                         a = g * 4 + j
                         out = None
                         for s in range(slots):
-                            first = starts[(q * slots + s) * na + o * ns + a]
+                            first = starts[q * slots + s, o * ns + a]
                             v = dr[a, pl.ds(first, TR // 8)].reshape(TR, 128)
                             out = v if s == 0 else jnp.where(lane == s, v, out)
                         tile[j * TR : (j + 1) * TR, :] = out
@@ -445,14 +470,7 @@
     for c in y_side:
         c.start()
     ymid[slab] = img[own_rows, MID0 : MID0 + MID]
-    own_out = [
-        pltpu.make_async_copy(img.at[own_rows, pl.ds(0, MID0)], res.at[slab, :, pl.ds(0, MID0)], s_loc.at[1]),
-        pltpu.make_async_copy(
-            img.at[own_rows, pl.ds(right0, rightn)], res.at[slab, :, pl.ds(right0, rightn)], s_loc.at[2]
-        ),
-    ]
-    for c in own_out:
-        c.start()
+    res[slab] = img[own_rows, :]
     for c in y_mid:
         c.wait()
     for g in range(quads):
@@ -460,10 +478,14 @@
         for h in range(MID // 128):
             yt[g, h * 128 : (h + 1) * 128, :] = jnp.transpose(block[:, h * 128 : (h + 1) * 128])
     end_forward(zs0, zr0, 0)
-    inverse = 1.0 / jnp.maximum(total_rays(zs0, zr0, quads), ROW_FLOOR)
-    inv_hi, inv_lo = split(inverse)
+    total = zsum[nz - 1]
+    for t in range(nz - 1):
+        total = total + zrsum[t]
+    inverse = 1.0 / jnp.maximum(total * (1.0 / ROI), ROW_FLOOR)
+    inv_hi, inv_lo = split(jnp.concatenate([inverse, jnp.zeros_like(inverse)], axis=0))
     for g in range(quads):
-        weight[g] = dot(inv_hi, copy_sum[g]) + dot(inv_lo, copy_sum[g])
+        weight[g] = (dot_tn(inv_hi, copy_sum[g]) + dot_tn(inv_lo, copy_sum[g]))[:RAYS]
+    for g in range(quads):
         dg[z, g] = (yt[g, SKIP : SKIP + RAYS, :] - total_rays(zs0, zr0, g)) * weight[g]
     d_out = spread(dg, 1)
     first = x0[...] + backward(dg, pv0, pr0, 1)
@@ -487,22 +509,21 @@
     d_out = spread(dh, 3)
     for g in range(quads):
         for h in range(MID // 128):
-            turned = jnp.transpose(yt[g, h * 128 : (h + 1) * 128, :])
-            rmid[g * 4 : (g + 1) * 4, :, h * 128 : (h + 1) * 128] = turned.reshape(4, 32, 128)
-    mid_out = pltpu.make_async_copy(rmid, res.at[:, :, pl.ds(MID0, MID)], s_loc.at[3])
-    mid_out.start()
-    rec[...] = first + backward(dh, pv1, pr1, 3)
+            turned = jnp.transpose(yt[g, h * 128 : (h + 1) * 128, :]).reshape(4, 32, 128)
+            res[g * 4 : (g + 1) * 4, :, MID0 + h * 128 : MID0 + (h + 1) * 128] = turned
+    last = first + backward(dh, pv1, pr1, 3)
+    for s in range(slots):
+        rec[:, s, :] = last[:, s * 256 : (s + 1) * 256]
     for c in d_out:
         c.wait_send()
 
-    mid_out.wait()
-    for c in own_out + y_side:
+    for c in y_side:
         c.wait()
 
 
-def sirt(starts, offs, cs, image, x0, dims):
+def sirt(starts, offs, cs, image, volume, dims):
     height, width = image.shape
-    h_hi, h_lo, table = filter_tables(height, width)
+    table = filter_tables(height, width)
     anywhere = pl.BlockSpec(memory_space=pl.ANY)
     ns, nz, nx = dims
     np_group = 4 * nx
@@ -518,31 +539,31 @@
         functools.partial(sirt_kernel, dims),
         out_shape=(
             jax.ShapeDtypeStruct((ns, 32, BAND), F32),
-            jax.ShapeDtypeStruct((32, 1024), F32),
+            jax.ShapeDtypeStruct(volume.shape, F32),
         ),
-        in_specs=[smem] * 3 + [anywhere] * 4 + [pl.BlockSpec(memory_space=pltpu.VMEM)],
-        out_specs=(pl.BlockSpec(memory_space=pl.ANY), pl.BlockSpec(memory_space=pltpu.VMEM)),
+        in_specs=[smem] * 3 + [anywhere, pl.BlockSpec(memory_space=pltpu.VMEM), anywhere],
+        out_specs=(pl.BlockSpec(memory_space=pltpu.VMEM), pl.BlockSpec(memory_space=pltpu.VMEM)),
         scratch_shapes=[
+            vm((32, 1024), F32),
             vm((height, width), F32),
             vm((height // 128, width + 2 * HALO, 128), F32),
             vm((height // 128, width + 2 * HALO, 128), F32),
-            vm(h_hi.shape, BF16),
-            vm(h_lo.shape, BF16),
-            vm(table.shape, F32),
+            vm((height, height), BF16),
+            vm((height, height), BF16),
             vm((RAYS, 512), BF16),
             vm((RAYS, 512), BF16),
-            vm((512, 128), BF16),
-            vm((quads, 512, 128), BF16),
+            vm((quads, 512, 256), BF16),
             vm((128, 512), BF16),
-            vm((quads, 128, 128), BF16),
+            vm((quads, 16, 128), BF16),
+            vm((RAYS, 128), F32),
             vm((np_group, rows, 256), BF16),
             vm((np_group, rows, 256), BF16),
             vm((np_group, 128, 256), BF16),
             vm((ns, (np_group * STRIDE + LEAD) // 8, 8, 128), F32),
             vm((nx, 32, 1024), F32),
             vm((nx, 32, 1024), F32),
-            vm((nz, quads + 1, RAYS, 128), F32),
-            vm((peers_z, quads + 1, RAYS, 128), F32),
+            vm((nz, quads, RAYS, 128), F32),
+            vm((peers_z, quads, RAYS, 128), F32),
             vm((nz, quads, RAYS, 128), F32),
             vm((peers_z, quads, RAYS, 128), F32),
             vm((nz, quads, RAYS, 128), F32),
@@ -557,7 +578,10 @@
             vm((ns, 32, MID), F32),
             vm((quads, MID, 128), F32),
             vm((quads, RAYS, 128), F32),
-            vm((ns, 32, MID), F32),
+            vm((nz, ns, 256), F32),
+            vm((peers_z, ns, 256), F32),
+            dma((peers_z,)),
+            dma((peers_z,)),
             dma((ns - 1,)),
             dma((ns - 1,)),
             dma((ns - 1,)),
@@ -571,34 +595,61 @@
             dma((8,)),
         ],
         compiler_params=pltpu.CompilerParams(
-            collective_id=0, has_side_effects=True, vmem_limit_bytes=62 << 20
+            collective_id=0, has_side_effects=True, vmem_limit_bytes=50 << 20
         ),
         name="sirt",
-    )(starts, offs, cs, image, jnp.asarray(h_hi), jnp.asarray(h_lo), jnp.asarray(table), x0)
-
-
-def tile_tables(angles, vol_list, z, x, nz, nx):
-    theta = lax.dynamic_index_in_dim(angles.reshape(-1, nz, nx), x, 2, keepdims=False)
-    theta = jnp.transpose(theta).reshape(-1)
-    ids = lax.dynamic_slice_in_dim(vol_list, z * 4 * nx, 4 * nx)
+    )(starts, offs, cs, image, jnp.asarray(table), volume)
+
+
+def tables_kernel(dims, angles, ids, starts, offs, cs):
+    ns, nz, nx = dims
+    ray = lax.axis_index("ray")
+    z = ray // nx
+    x = lax.rem(ray, nx)
+    shape = (4 * nx, 128)
+    row = lax.broadcasted_iota(jnp.int32, shape, 0)
+    lane = lax.broadcasted_iota(jnp.int32, shape, 1)
+    theta = jnp.zeros(shape, F32)
+    for a in range(ns * nz):
+        theta = jnp.where(lane == a, angles[a % ns, a // ns * nx + x], theta)
+    patch = jnp.zeros(shape, jnp.int32)
+    for p in range(4 * nx):
+        patch = jnp.where(row == p, ids[z * 4 * nx + p], patch)
     cosine = jnp.cos(theta)
     sine = jnp.sin(theta)
-    centre_x = (ids // PGRID).astype(F32) * 16.0 + 7.5 - HALF_ROI
-    centre_y = (ids % PGRID).astype(F32) * 16.0 + 7.5 - HALF_ROI
-    centre = HALF_BAND + centre_x[:, None] * cosine[None, :] + centre_y[:, None] * sine[None, :]
+    centre_x = (patch // PGRID).astype(F32) * 16.0 + 7.5 - HALF_ROI
+    centre_y = (patch % PGRID).astype(F32) * 16.0 + 7.5 - HALF_ROI
+    centre = HALF_BAND + centre_x * cosine + centre_y * sine
     first = jnp.floor(centre - 11.61).astype(jnp.int32) + 1
     start = first // 8
-    offs = (start * 8).astype(F32) - centre
-    return (start - RAY0 // 8).reshape(-1), offs.reshape(-1), jnp.concatenate([cosine, sine])
+    starts[...] = start - RAY0 // 8
+    offs[...] = (start * 8).astype(F32) - centre
+    cs[0:8, :] = cosine[0:8]
+    cs[8:16, :] = sine[0:8]
+
+
+def tile_tables(angles, vol_list, dims):
+    shape = (4 * dims[2], 128)
+    return pl.pallas_call(
+        functools.partial(tables_kernel, dims),
+        out_shape=(
+            jax.ShapeDtypeStruct(shape, jnp.int32),
+            jax.ShapeDtypeStruct(shape, F32),
+            jax.ShapeDtypeStruct((16, 128), F32),
+        ),
+        in_specs=[pl.BlockSpec(memory_space=pltpu.SMEM)] * 2,
+        out_specs=(pl.BlockSpec(memory_space=pltpu.VMEM),) * 3,
+        compiler_params=pltpu.CompilerParams(vmem_limit_bytes=4 << 20),
+        name="tile_tables",
+    )(angles, vol_list)
 
 
 def local(dims, intensity, angles, volume, vol_list):
     ns, nz, nx = dims
-    rank = lax.axis_index("ray")
     height = intensity.shape[2]
-    starts, offs, cs = tile_tables(angles, vol_list, rank // nx, rank % nx, nz, nx)
-    res, rec = sirt(starts, offs, cs, intensity.reshape(height, BAND), volume.reshape(32, 1024), dims)
-    return rec.reshape(volume.shape), res[:, None]
+    starts, offs, cs = tile_tables(angles, vol_list, dims)
+    res, rec = sirt(starts, offs, cs, intensity.reshape(height, BAND), volume, dims)
+    return rec, res[:, None]
 
 
 def make(mesh, dims):

time: 124 us -> 114 us (0.919)
  Pallas kernels: 113 us -> 107 us
  other arithmetic: 2.68 us -> 0 us
  local copies, waits for them, and re-layouts: 7.42 us -> 5.17 us
    pallas_call x1, Pallas kernels: 113 us -> 107 us  [sirt(): pl.pallas_call(functools.partial(sirt_kernel, dims), out_shape=(jax.Shape...]
    sub x4 -> x0, other arithmetic: 1.95 us -> none  [the longest x1 0.74 us: tile_tables(): centre_x = (ids // PGRID).astype(F32) * 16.0 + 7.5 - HALF_ROI]
    reshape x1 -> x0, local copies, waits for them, and re-layouts: 1.62 us -> none  [local(): return (rec.reshape(volume.shape), res[:, None])]
    unnamed x3 -> x10, local copies, waits for them, and re-layouts: 5.48 us -> 5.17 us
where the time goes in v3:
time: 114 us; the launch traced here: 113 us
  Pallas kernels  107 us (94%)
  local copies, waits for them, and re-layouts  5.17 us (5%)
    pallas_call x1, Pallas kernels, sirt(): pl.pallas_call(functools.partial(sirt_kernel, dims), out_shape=(jax.Shape...  107 us
    unnamed x10, local copies, waits for them, and re-layouts  5.17 us

profile of v3, /device:TPU:0, one launch (start us, length us, event | category | flops | bytes accessed | tf_op | source)
XLA Modules:
  0.0 113.2 jit_solution(1642851768889505776)
XLA Ops:
  0.6 0.0 copy-start.2
  0.6 0.7 copy-done.2
  1.3 0.0 copy-start.3
  1.3 0.7 copy-done.3
  2.0 0.7 tile_tables.1
  2.7 0.0 copy-start
  2.7 0.9 copy-done
  3.6 0.0 copy-start.1
  3.6 0.9 copy-done.1
  4.5 106.6 %sirt.1 = (f32[8,32,2048]{2,1,0:T(8,128)S(1)}, f32[32,4,256]{2,1,0:T(4,128)S(1)}) custom-call(s32[16,128]{1,0:T(8,128)S(1)} %get-tuple-element.7.starts, f32[16,128]{1,0:T(8,128)S(1)} %get-tuple-element.8.offs, f32[16,128]{1,0:T(8,128)S(1)} %get-tuple-element.9.cs, f32[256,2048]{1,0:T(8,128)} %bitcast.5, f32[272,256]{1,0:T(8,128)S(1)} %copy-done, ...), custom_call_target="tpu_custom_call" | custom-call | tf_op jit(solution)/shard_map/sirt/pallas_call | solution.py:538
  111.2 0.7 copy.10
  111.8 1.3 %copy.11 = f32[8,1,32,2048]{3,2,1,0:T(8,128)} copy(f32[8,1,32,2048]{3,2,1,0:T(8,128)S(1)} %bitcast.4) | data formatting | bytes 4194304
Async XLA Ops:
  0.6 0.7 copy-start.2
  1.3 0.7 copy-start.3
  2.7 1.0 copy-start
  3.6 0.9 copy-start.1

commit v4 on v3

--- a/solution.py
+++ b/solution.py
@@ -315,27 +315,57 @@
         copy_sum[g] = one_hot((16, 128), lambda r, c, g=g: r == g * 4 + c // 32)
     copy_out[...] = one_hot((128, 512), lambda r, c: (r // 32 == c // 128) & (r % 32 == c % 32))
 
-    def load_volume(source):
-        for q in range(nx):
-            for s in range(slots):
-                hi, lo = split(source[q, :, pl.ds(s * 256, 256)])
-                xb[q * slots + s, 0:32, :] = hi
-                xb[q * slots + s, 32:64, :] = lo
+    def load_shard(source, q):
+        for s in range(slots):
+            hi, lo = split(source[q, :, pl.ds(s * 256, 256)])
+            xb[q * slots + s, 0:32, :] = hi
+            xb[q * slots + s, 32:64, :] = lo
+
+    def ahead(t):
+        return 2 - t + 3 * (t // 2) + 2 * (t // 3)
+
+    def behind(t):
+        return t + t // 2 - 2 * (t // 3)
 
     def forward(zs, zr, phase):
         with_sums = phase == 0
 
         @pl.loop(0, nz)
         def _(t):
-            o = lax.rem(z + 1 + t, nz)
+            o = lax.rem(z + ahead(t), nz)
             rows = pl.ds(pl.multiple_of(o * (ns * TR), ns * TR), ns * TR)
 
-            @pl.loop(0, np_group, unroll=8)
-            def _(p):
+            def weigh(p):
                 part = dot_nt(w_hi[p, rows, :], xb[p]) + dot_nt(w_lo[p, rows, :], xb[p])
                 at = pl.ds(p * (STRIDE // 8) + LEAD // 8, TR // 8)
                 for a in range(ns):
                     pad[a, at] = part[a * TR : (a + 1) * TR].reshape(TR // 8, 8, 128)
+
+            def weigh_all():
+                @pl.loop(0, np_group, unroll=8)
+                def _(p):
+                    weigh(p)
+
+            if phase == 0:
+                weigh_all()
+            else:
+                pl.when(t > 0)(weigh_all)
+
+                @pl.when(t == 0)
+                def _():
+                    @pl.loop(0, nx)
+                    def _(u):
+                        off = behind(u)
+                        q = lax.rem(x + nx - off, nx)
+
+                        @pl.when(u > 0)
+                        def _():
+                            part = xh.at[q]
+                            send(part, part, s_x.at[2, off - 1], r_x.at[2, off - 1], at_x(1)).wait_recv()
+
+                        load_shard(xh, q)
+                        for s in range(slots):
+                            weigh(q * slots + s)
 
             @pl.loop(0, quads)
             def _(g):
@@ -362,9 +392,9 @@
 
             @pl.when(t < nz - 1)
             def _():
-                send(zs.at[t], zr.at[t], s_z.at[phase, t], r_z.at[phase, t], at_z(1 + t)).start()
+                send(zs.at[t], zr.at[t], s_z.at[phase, t], r_z.at[phase, t], at_z(ahead(t))).start()
                 if with_sums:
-                    send(zsum.at[t], zrsum.at[t], s_sum.at[t], r_sum.at[t], at_z(1 + t)).start()
+                    send(zsum.at[t], zrsum.at[t], s_sum.at[t], r_sum.at[t], at_z(ahead(t))).start()
 
     def end_forward(zs, zr, phase):
         for t in range(nz - 1):
@@ -396,7 +426,7 @@
 
         @pl.loop(0, nz)
         def _(t):
-            off = t + t // 2 - 2 * (t // 3)
+            off = behind(t)
             o = lax.rem(z + nz - off, nz)
 
             @pl.when(t > 0)
@@ -413,7 +443,7 @@
 
             @pl.loop(0, nx)
             def _(u):
-                q = lax.rem(x + 1 + u, nx)
+                q = lax.rem(x + ahead(u), nx)
                 for g in range(quads):
                     for j in range(4):
                         a = g * 4 + j
@@ -436,7 +466,7 @@
 
                 @pl.when((t == nz - 1) & (u < nx - 1))
                 def _():
-                    send(pv.at[u], pr.at[u], s_x.at[phase, u], r_x.at[phase, u], at_x(1 + u)).start()
+                    send(pv.at[u], pr.at[u], s_x.at[phase, u], r_x.at[phase, u], at_x(ahead(u))).start()
 
         for t in range(nx - 1):
             c = send(pv.at[t], pr.at[t], s_x.at[phase, t], r_x.at[phase, t], at_x(1 + t))
@@ -451,15 +481,17 @@
         c.wait()
     modes = filter_forward(img, h_hi, h_lo, table, ping, pong)
 
+    filter_back(modes, h_hi, h_lo, img, MID0, MID)
+    for c in y_mid:
+        c.start()
+
     xg[x] = x0[...]
     for c in x_out:
         c.wait()
-    load_volume(xg)
+    for q in range(nx):
+        load_shard(xg, q)
     forward(zs0, zr0, 0)
 
-    filter_back(modes, h_hi, h_lo, img, MID0, MID)
-    for c in y_mid:
-        c.start()
     for base in (0, right0):
 
         @pl.loop(0, 3)
@@ -497,10 +529,9 @@
     ]
     for c in x_out:
         c.start()
+    forward(zs1, zr1, 2)
     for c in x_out:
-        c.wait()
-    load_volume(xh)
-    forward(zs1, zr1, 2)
+        c.wait_send()
     end_forward(zs1, zr1, 2)
     for g in range(quads):
         diff = yt[g, SKIP : SKIP + RAYS, :] - total_rays(zs1, zr1, g)

time: 114 us -> 110 us (0.965)
  Pallas kernels: 107 us -> 102 us
    pallas_call x1, Pallas kernels: 107 us -> 102 us  [sirt(): pl.pallas_call(functools.partial(sirt_kernel, dims), out_shape=(jax.Shape...]
where the time goes in v4:
time: 110 us; the launch traced here: 108 us
  Pallas kernels  102 us (93%)
  local copies, waits for them, and re-layouts  5.17 us (5%)
    pallas_call x1, Pallas kernels, sirt(): pl.pallas_call(functools.partial(sirt_kernel, dims), out_shape=(jax.Shape...  102 us
    unnamed x10, local copies, waits for them, and re-layouts  5.17 us

profile of v4, /device:TPU:0, one launch (start us, length us, event | category | flops | bytes accessed | tf_op | source)
XLA Modules:
  0.0 108.3 jit_solution(920014782965601956)
XLA Ops:
  0.6 0.0 copy-start.2
  0.6 0.7 copy-done.2
  1.3 0.0 copy-start.3
  1.3 0.7 copy-done.3
  2.0 0.7 tile_tables.1
  2.7 0.0 copy-start
  2.7 0.9 copy-done
  3.6 0.0 copy-start.1
  3.6 0.9 copy-done.1
  4.5 101.8 %sirt.1 = (f32[8,32,2048]{2,1,0:T(8,128)S(1)}, f32[32,4,256]{2,1,0:T(4,128)S(1)}) custom-call(s32[16,128]{1,0:T(8,128)S(1)} %get-tuple-element.7.starts, f32[16,128]{1,0:T(8,128)S(1)} %get-tuple-element.8.offs, f32[16,128]{1,0:T(8,128)S(1)} %get-tuple-element.9.cs, f32[256,2048]{1,0:T(8,128)} %bitcast.5, f32[272,256]{1,0:T(8,128)S(1)} %copy-done, ...), custom_call_target="tpu_custom_call" | custom-call | tf_op jit(solution)/shard_map/sirt/pallas_call | solution.py:569
  106.3 0.7 copy.10
  107.0 1.3 %copy.11 = f32[8,1,32,2048]{3,2,1,0:T(8,128)} copy(f32[8,1,32,2048]{3,2,1,0:T(8,128)S(1)} %bitcast.4) | data formatting | bytes 4194304
Async XLA Ops:
  0.6 0.7 copy-start.2
  1.3 0.7 copy-start.3
  2.7 1.0 copy-start
  3.6 0.9 copy-start.1

commit v5 on v4

--- a/solution.py
+++ b/solution.py
@@ -21,8 +21,8 @@
 TR = 32
 MID0 = 896
 MID = 256
-RAY0 = 928
-RAYS = 192
+RAY0 = 932
+RAYS = 184
 SKIP = RAY0 - MID0
 STRIDE = RAYS
 LEAD = RAYS - TR
@@ -315,11 +315,13 @@
         copy_sum[g] = one_hot((16, 128), lambda r, c, g=g: r == g * 4 + c // 32)
     copy_out[...] = one_hot((128, 512), lambda r, c: (r // 32 == c // 128) & (r % 32 == c % 32))
 
-    def load_shard(source, q):
+    def load_shard(source, q, copies):
         for s in range(slots):
             hi, lo = split(source[q, :, pl.ds(s * 256, 256)])
-            xb[q * slots + s, 0:32, :] = hi
-            xb[q * slots + s, 32:64, :] = lo
+            for k in range(copies):
+                xb[q * slots + s, k * 32 : (k + 1) * 32, :] = hi
+                low = (k + copies) * 32
+                xb[q * slots + s, low : low + 32, :] = lo
 
     def ahead(t):
         return 2 - t + 3 * (t // 2) + 2 * (t // 3)
@@ -336,13 +338,16 @@
             rows = pl.ds(pl.multiple_of(o * (ns * TR), ns * TR), ns * TR)
 
             def weigh(p):
-                part = dot_nt(w_hi[p, rows, :], xb[p]) + dot_nt(w_lo[p, rows, :], xb[p])
+                wide = xb[p, 0:128] if with_sums else xb[p]
+                part = dot_nt(w_hi[p, rows, :], wide) + dot_nt(w_lo[p, rows, :], wide)
+                if not with_sums:
+                    part = part[:, :128] + part[:, 128:]
                 at = pl.ds(p * (STRIDE // 8) + LEAD // 8, TR // 8)
                 for a in range(ns):
                     pad[a, at] = part[a * TR : (a + 1) * TR].reshape(TR // 8, 8, 128)
 
             def weigh_all():
-                @pl.loop(0, np_group, unroll=8)
+                @pl.loop(0, np_group, unroll=16 if with_sums else 8)
                 def _(p):
                     weigh(p)
 
@@ -363,27 +368,31 @@
                             part = xh.at[q]
                             send(part, part, s_x.at[2, off - 1], r_x.at[2, off - 1], at_x(1)).wait_recv()
 
-                        load_shard(xh, q)
+                        load_shard(xh, q, 4)
                         for s in range(slots):
                             weigh(q * slots + s)
 
             @pl.loop(0, quads)
             def _(g):
+                packed = jnp.zeros((RAYS, 128), F32)
                 for i in range(4):
                     a = g * 4 + i
                     acc = jnp.zeros((RAYS, 128), F32)
                     for p in range(np_group):
                         first = (p * STRIDE + LEAD) // 8 - starts[p, o * ns + a]
                         acc = acc + pad[a, pl.ds(first, RAYS // 8)].reshape(RAYS, 128)
-                    hi, lo = split(acc)
-                    parts_hi[:, i * 128 : (i + 1) * 128] = hi
-                    parts_lo[:, i * 128 : (i + 1) * 128] = lo
+                    if with_sums:
+                        hi, lo = split(acc)
+                        parts_hi[0:RAYS, i * 128 : (i + 1) * 128] = hi
+                        parts_lo[0:RAYS, i * 128 : (i + 1) * 128] = lo
+                    else:
+                        packed = jnp.where(lane == i, acc, packed)
                 if with_sums:
-                    part = dot(parts_hi[...], pick[g]) + dot(parts_lo[...], pick[g])
+                    part = dot(parts_hi[0:RAYS], pick[g]) + dot(parts_lo[0:RAYS], pick[g])
                     zs[t, g] = part[:, :128]
                     sums[...] = jnp.where(g == 0, part[:, 128:], part[:, 128:] + sums[...])
                 else:
-                    zs[t, g] = dot(parts_hi[...], pick[0, :, 0:128]) + dot(parts_lo[...], pick[0, :, 0:128])
+                    zs[t, g] = packed
 
             if with_sums:
                 zsum[t, :, 0:128] = jnp.transpose(sums[0:128])[0:ns]
@@ -489,7 +498,7 @@
     for c in x_out:
         c.wait()
     for q in range(nx):
-        load_shard(xg, q)
+        load_shard(xg, q, 1)
     forward(zs0, zr0, 0)
 
     for base in (0, right0):
@@ -581,15 +590,15 @@
             vm((height // 128, width + 2 * HALO, 128), F32),
             vm((height, height), BF16),
             vm((height, height), BF16),
-            vm((RAYS, 512), BF16),
-            vm((RAYS, 512), BF16),
+            vm((192, 512), BF16),
+            vm((192, 512), BF16),
             vm((quads, 512, 256), BF16),
             vm((128, 512), BF16),
             vm((quads, 16, 128), BF16),
             vm((RAYS, 128), F32),
             vm((np_group, rows, 256), BF16),
             vm((np_group, rows, 256), BF16),
-            vm((np_group, 128, 256), BF16),
+            vm((np_group, 256, 256), BF16),
             vm((ns, (np_group * STRIDE + LEAD) // 8, 8, 128), F32),
             vm((nx, 32, 1024), F32),
             vm((nx, 32, 1024), F32),
@@ -626,7 +635,7 @@
             dma((8,)),
         ],
         compiler_params=pltpu.CompilerParams(
-            collective_id=0, has_side_effects=True, vmem_limit_bytes=50 << 20
+            collective_id=0, has_side_effects=True, vmem_limit_bytes=51 << 20
         ),
         name="sirt",
     )(starts, offs, cs, image, jnp.asarray(table), volume)
@@ -652,9 +661,9 @@
     centre_y = (patch % PGRID).astype(F32) * 16.0 + 7.5 - HALF_ROI
     centre = HALF_BAND + centre_x * cosine + centre_y * sine
     first = jnp.floor(centre - 11.61).astype(jnp.int32) + 1
-    start = first // 8
-    starts[...] = start - RAY0 // 8
-    offs[...] = (start * 8).astype(F32) - centre
+    start = jnp.minimum((first - RAY0) // 8, (RAYS - TR) // 8)
+    starts[...] = start
+    offs[...] = (start * 8 + RAY0).astype(F32) - centre
     cs[0:8, :] = cosine[0:8]
     cs[8:16, :] = sine[0:8]
 

time: 110 us -> 108 us (0.982); the launches traced: 108 us -> 107 us
  no operation moved by 1% of the time
where the time goes in v5:
time: 108 us; the launch traced here: 107 us
  Pallas kernels  102 us (94%)
  local copies, waits for them, and re-layouts  5.17 us (5%)
    pallas_call x1, Pallas kernels, sirt(): pl.pallas_call(functools.partial(sirt_kernel, dims), out_shape=(jax.Shape...  101 us
    unnamed x10, local copies, waits for them, and re-layouts  5.17 us

profile of v5, /device:TPU:0, one launch (start us, length us, event | category | flops | bytes accessed | tf_op | source)
XLA Modules:
  0.0 107.5 jit_solution(9510680439433581671)
XLA Ops:
  0.6 0.0 copy-start.2
  0.6 0.7 copy-done.2
  1.3 0.0 copy-start.3
  1.3 0.7 copy-done.3
  2.0 0.7 tile_tables.1
  2.7 0.0 copy-start
  2.7 0.9 copy-done
  3.6 0.0 copy-start.1
  3.6 0.9 copy-done.1
  4.6 100.9 %sirt.1 = (f32[8,32,2048]{2,1,0:T(8,128)S(1)}, f32[32,4,256]{2,1,0:T(4,128)S(1)}) custom-call(s32[16,128]{1,0:T(8,128)S(1)} %get-tuple-element.7.starts, f32[16,128]{1,0:T(8,128)S(1)} %get-tuple-element.8.offs, f32[16,128]{1,0:T(8,128)S(1)} %get-tuple-element.9.cs, f32[256,2048]{1,0:T(8,128)} %bitcast.5, f32[272,256]{1,0:T(8,128)S(1)} %copy-done, ...), custom_call_target="tpu_custom_call" | custom-call | tf_op jit(solution)/shard_map/sirt/pallas_call | solution.py:578
  105.5 0.7 copy.10
  106.1 1.3 %copy.11 = f32[8,1,32,2048]{3,2,1,0:T(8,128)} copy(f32[8,1,32,2048]{3,2,1,0:T(8,128)S(1)} %bitcast.4) | data formatting | bytes 4194304
Async XLA Ops:
  0.6 0.7 copy-start.2
  1.3 0.7 copy-start.3
  2.7 1.0 copy-start
  3.6 0.9 copy-start.1

commit v6 on v5

--- a/solution.py
+++ b/solution.py
@@ -408,12 +408,14 @@
     def end_forward(zs, zr, phase):
         for t in range(nz - 1):
             c = send(zs.at[t], zr.at[t], s_z.at[phase, t], r_z.at[phase, t], at_z(1 + t))
-            c.wait_send()
+            late.append(c)
             c.wait_recv()
             if phase == 0:
                 c = send(zsum.at[t], zrsum.at[t], s_sum.at[t], r_sum.at[t], at_z(1 + t))
-                c.wait_send()
+                late.append(c)
                 c.wait_recv()
+
+    late = []
 
     def total_rays(zs, zr, index):
         v = zs[nz - 1, index]
@@ -479,7 +481,7 @@
 
         for t in range(nx - 1):
             c = send(pv.at[t], pr.at[t], s_x.at[phase, t], r_x.at[phase, t], at_x(1 + t))
-            c.wait_send()
+            late.append(c)
             c.wait_recv()
         v = pv[nx - 1]
         for t in range(nx - 1):
@@ -530,8 +532,7 @@
         dg[z, g] = (yt[g, SKIP : SKIP + RAYS, :] - total_rays(zs0, zr0, g)) * weight[g]
     d_out = spread(dg, 1)
     first = x0[...] + backward(dg, pv0, pr0, 1)
-    for c in d_out:
-        c.wait_send()
+    late.extend(d_out)
     xh[x] = first
     x_out = [
         send(xh.at[x], xh.at[x], s_x.at[2, t - 1], r_x.at[2, t - 1], at_x(t)) for t in range(1, nx)
@@ -539,8 +540,7 @@
     for c in x_out:
         c.start()
     forward(zs1, zr1, 2)
-    for c in x_out:
-        c.wait_send()
+    late.extend(x_out)
     end_forward(zs1, zr1, 2)
     for g in range(quads):
         diff = yt[g, SKIP : SKIP + RAYS, :] - total_rays(zs1, zr1, g)
@@ -554,11 +554,12 @@
     last = first + backward(dh, pv1, pr1, 3)
     for s in range(slots):
         rec[:, s, :] = last[:, s * 256 : (s + 1) * 256]
-    for c in d_out:
-        c.wait_send()
+    late.extend(d_out)
 
     for c in y_side:
         c.wait()
+    for c in late:
+        c.wait_send()
 
 
 def sirt(starts, offs, cs, image, volume, dims):

time: 108 us -> 108 us (level)
  no operation moved by 1% of the time
where the time goes in v6:
time: 108 us; the launch traced here: 107 us
  Pallas kernels  101 us (94%)
  local copies, waits for them, and re-layouts  5.17 us (5%)
    pallas_call x1, Pallas kernels, sirt(): pl.pallas_call(functools.partial(sirt_kernel, dims), out_shape=(jax.Shape...  100 us
    unnamed x10, local copies, waits for them, and re-layouts  5.17 us

profile of v6, /device:TPU:0, one launch (start us, length us, event | category | flops | bytes accessed | tf_op | source)
XLA Modules:
  0.0 107.0 jit_solution(7158211569878847313)
XLA Ops:
  0.6 0.0 copy-start.2
  0.6 0.7 copy-done.2
  1.3 0.0 copy-start.3
  1.3 0.7 copy-done.3
  2.0 0.7 tile_tables.1
  2.7 0.0 copy-start
  2.7 0.9 copy-done
  3.6 0.0 copy-start.1
  3.6 0.9 copy-done.1
  4.6 100.5 %sirt.1 = (f32[8,32,2048]{2,1,0:T(8,128)S(1)}, f32[32,4,256]{2,1,0:T(4,128)S(1)}) custom-call(s32[16,128]{1,0:T(8,128)S(1)} %get-tuple-element.7.starts, f32[16,128]{1,0:T(8,128)S(1)} %get-tuple-element.8.offs, f32[16,128]{1,0:T(8,128)S(1)} %get-tuple-element.9.cs, f32[256,2048]{1,0:T(8,128)} %bitcast.5, f32[272,256]{1,0:T(8,128)S(1)} %copy-done, ...), custom_call_target="tpu_custom_call" | custom-call | tf_op jit(solution)/shard_map/sirt/pallas_call | solution.py:579
  105.0 0.7 copy.10
  105.7 1.3 %copy.11 = f32[8,1,32,2048]{3,2,1,0:T(8,128)} copy(f32[8,1,32,2048]{3,2,1,0:T(8,128)S(1)} %bitcast.4) | data formatting | bytes 4194304
Async XLA Ops:
  0.6 0.7 copy-start.2
  1.3 0.7 copy-start.3
  2.7 1.0 copy-start
  3.6 0.9 copy-start.1
